TPU v7x, 32 devices: a whole 2x2x4 slice. The times are simulated.
32 devices in a mesh: grp: 2 (over y), ia: 4 (over z), ja: 4 (over x, core).
Axes of the slice: x: 2, y: 2, z: 4, core: 2. Of those that a mesh axis runs over, the one named last changes fastest.
Arguments:
- doubles: bfloat16 [8, 16, 384, 384], P(('grp', 'ia'), 'ja'), parts along dimension 0, may hold values from -6 to 6
- aux_factors: bfloat16 [4, 384, 384], P('ia'), may hold values from -0.15625 to 0.15625
- cycle_factors: bfloat16 [16, 384, 128], replicated, may hold values from -0.21875 to 0.21875
Outputs:
- sigma: bfloat16 [8, 16, 384, 384], P(('grp', 'ia'), 'ja'), parts along dimension 0
There are 2 independent parts, one for each index of `grp`. A program takes and returns all parts, laid end to end along the dimension named above; an argument that names none is the same for every part. Nothing has to cross between parts.
All inputs are finite; a program needn't handle non-finite values.
Results may differ from a plain program's by a relative error of at most 0.008.
Values may be sent and summed in bfloat16 or wider, within the bound.
No kernel may reach another device: no remote copies, remote signals or barrier semaphores. Data moves between devices by JAX's collectives and lax.ppermute only.
A program may use at most 128 MiB of HBM per device.

v0:
```python
import jax
import jax.numpy as jnp
from jax import lax
from jax.sharding import PartitionSpec as P


def ladder_terms(pair_blocks, factor):
    halfway = jnp.einsum(
        "pcd,bd->pcb", pair_blocks, factor, preferred_element_type=jnp.float32
    ).astype(jnp.bfloat16)
    return jnp.einsum("ac,pcb->pab", factor, halfway, preferred_element_type=jnp.float32)


def add_factors(running, pair_blocks, factors):

    def one_step(position, acc):
        factor = lax.dynamic_index_in_dim(factors, position, 0, keepdims=False)
        return acc + ladder_terms(pair_blocks, factor)

    return lax.fori_loop(0, factors.shape[0], one_step, running)


def shards(doubles, aux_factors, cycle_factors):
    rows_i, cols_j, width, _ = doubles.shape
    pair_blocks = doubles.reshape(rows_i * cols_j, width, width)
    zeros_acc = jnp.zeros((rows_i * cols_j, width, width), jnp.float32)
    ladder = add_factors(
        zeros_acc, pair_blocks, lax.all_gather(aux_factors, "ia", axis=0, tiled=True)
    )
    ladder = ladder.reshape(rows_i, cols_j, width, width)
    offset = lax.axis_index("ja") * cols_j
    local_factors = lax.dynamic_slice_in_dim(cycle_factors, offset, cols_j, 0)
    partial_latent = jnp.einsum(
        "ijab,jbq->iaq", doubles, local_factors, preferred_element_type=jnp.float32
    )
    latent = lax.psum(partial_latent, "ja").astype(jnp.bfloat16)
    cycle_term = jnp.einsum(
        "iaq,jbq->ijab", latent, local_factors, preferred_element_type=jnp.float32
    ).astype(jnp.bfloat16)
    return (ladder + cycle_term.astype(jnp.float32)).astype(jnp.bfloat16)


def solution(mesh):
    in_specs = (P(("grp", "ia"), "ja", None, None), P("ia", None, None), P())
    out_specs = P(("grp", "ia"), "ja", None, None)
    return jax.shard_map(shards, mesh=mesh, in_specs=in_specs, out_specs=out_specs, check_vma=False)
```

profile of v0, /device:TPU:0, one launch (start us, length us, event | category | flops | bytes accessed | tf_op | source)
XLA Modules:
  0.0 70.7 jit_solution(2368934704128992936)
XLA Ops:
  6.5 0.0 copy-start
  6.5 0.0 copy-start.1
  6.5 0.0 all-gather.2.cloned.1.call-start
  6.5 0.7 %all-gather.2.cloned.1.call-update = ((bf16[1,384,384]{2,1,0:T(8,128)(2,1)}), bf16[4,384,384]{2,1,0:T(8,128)(2,1)}) async-update(((), (), s32[]{:S(2)}) %all-gather.2.cloned.1.call-start, bf16[1,384,384]{2,1,0:T(8,128)(2,1)} %param.6) | async-update | bytes 1769496
  7.3 0.7 copy-done
  7.9 1.8 %convolution_bitcast_fusion = f32[1,384,128]{1,2,0:T(8,128)S(1)} fusion(bf16[16,384,128]{2,1,0:T(8,128)(2,1)S(1)} %copy-done, s32[]{:T(128)S(6)} %select_n.9, bf16[1,4,384,384]{3,2,1,0:T(8,128)(2,1)} %param.5), kind=kOutput, calls=%fused_computation.11 | convolution fusion | flops 150994944 | bytes 1769476 | tf_op jit(solution)/shard_map/ijab,jbq->iaq/dot_general | solution.py:33
  9.7 15.3 %all-reduce.1 = bf16[1,384,128]{1,2,0:T(8,128)(2,1)S(1)} all-reduce(f32[1,384,128]{1,2,0:T(8,128)S(1)} %convolution_bitcast_fusion), channel_id=1, replica_groups=mesh['grp'=2,'ia'=4,'ja'=4] {'ja'}, use_global_device_ids=true, to_apply=%region_2.3 | all-reduce | flops 49152 | bytes 294912 | tf_op jit(solution)/shard_map/psum | solution.py:36
  25.0 16.9 %all-gather.2.cloned.1.call-done = bf16[4,384,384]{2,1,0:T(8,128)(2,1)} async-done(((bf16[1,384,384]{2,1,0:T(8,128)(2,1)}), bf16[4,384,384]{2,1,0:T(8,128)(2,1)}) %all-gather.2.cloned.1.call-update) | async-done | bytes 1179664 | tf_op jit(solution)/shard_map/all_gather | solution.py:28
  41.9 0.0 copy-done.1
  41.9 18.4 %while.14 = (s32[]{:T(128)}, f32[4,384,384]{1,2,0:T(8,128)}, bf16[4,384,384]{2,1,0:T(8,128)(2,1)}, bf16[4,384,384]{2,1,0:T(8,128)(2,1)S(1)}, s32[]{:T(128)}, /*index=5*/s32[]{:T(128)}) while((s32[]{:T(128)}, f32[4,384,384]{1,2,0:T(8,128)}, bf16[4,384,384]{2,1,0:T(8,128)(2,1)}, bf16[4,384,384]{2,1,0:T(8,128)(2,1)S(1)}, s32[]{:T(128)}, ...), condition=%wide.region_1.2_spmd.clone, body=%wide.region_0.1_spmd.clone.sunk | while | flops 907739136 | bytes 6489686 | solution.py:20
  41.9 4.0 %bitcast_add_fusion.2 = f32[4,384,384]{1,2,0:T(8,128)} fusion(f32[4,384,384]{1,2,0:T(8,128)} %get-tuple-element.140, bf16[4,384,384]{2,1,0:T(8,128)(2,1)S(1)} %get-tuple-element.148, pred[]{:T(512)S(6)} %compare.3, bf16[4,384,384]{2,1,0:T(8,128)(2,1)} %get-tuple-element.147, s32[]{:T(128)S(6)} %copy.18), kind=kOutput, calls=%fused_computation.clone.1 | convolution fusion | flops 907739136 | bytes 6489600 | tf_op jit(solution)/shard_map/while/body/eval_jaxpr/ac,pcb->pab/dot_general | solution.py:11
  45.9 4.8 %bitcast_add_fusion.2 = f32[4,384,384]{1,2,0:T(8,128)} fusion(f32[4,384,384]{1,2,0:T(8,128)} %get-tuple-element.140, bf16[4,384,384]{2,1,0:T(8,128)(2,1)S(1)} %get-tuple-element.148, pred[]{:T(512)S(6)} %compare.3, bf16[4,384,384]{2,1,0:T(8,128)(2,1)} %get-tuple-element.147, s32[]{:T(128)S(6)} %copy.18), kind=kOutput, calls=%fused_computation.clone.1 | convolution fusion | flops 907739136 | bytes 6489600 | tf_op jit(solution)/shard_map/while/body/eval_jaxpr/ac,pcb->pab/dot_general | solution.py:11
  50.7 4.8 %bitcast_add_fusion.2 = f32[4,384,384]{1,2,0:T(8,128)} fusion(f32[4,384,384]{1,2,0:T(8,128)} %get-tuple-element.140, bf16[4,384,384]{2,1,0:T(8,128)(2,1)S(1)} %get-tuple-element.148, pred[]{:T(512)S(6)} %compare.3, bf16[4,384,384]{2,1,0:T(8,128)(2,1)} %get-tuple-element.147, s32[]{:T(128)S(6)} %copy.18), kind=kOutput, calls=%fused_computation.clone.1 | convolution fusion | flops 907739136 | bytes 6489600 | tf_op jit(solution)/shard_map/while/body/eval_jaxpr/ac,pcb->pab/dot_general | solution.py:11
  55.5 4.8 %bitcast_add_fusion.2 = f32[4,384,384]{1,2,0:T(8,128)} fusion(f32[4,384,384]{1,2,0:T(8,128)} %get-tuple-element.140, bf16[4,384,384]{2,1,0:T(8,128)(2,1)S(1)} %get-tuple-element.148, pred[]{:T(512)S(6)} %compare.3, bf16[4,384,384]{2,1,0:T(8,128)(2,1)} %get-tuple-element.147, s32[]{:T(128)S(6)} %copy.18), kind=kOutput, calls=%fused_computation.clone.1 | convolution fusion | flops 907739136 | bytes 6489600 | tf_op jit(solution)/shard_map/while/body/eval_jaxpr/ac,pcb->pab/dot_general | solution.py:11
  60.3 2.1 %fusion.8 = bf16[1,4,384,384]{2,3,1,0:T(8,128)(2,1)S(1)} fusion(f32[4,384,384]{1,2,0:T(8,128)} %get-tuple-element.84, bf16[16,384,128]{2,1,0:T(8,128)(2,1)S(1)} %copy-done, s32[]{:T(128)S(6)} %select_n.9, bf16[1,384,128]{1,2,0:T(8,128)(2,1)S(1)} %all-reduce.1), kind=kOutput, calls=%fused_computation.8 | convolution fusion | flops 153354240 | bytes 4030468 | tf_op jit(solution)/shard_map/iaq,jbq->ijab/dot_general | solution.py:37
  62.4 1.5 %copy.11 = bf16[1,4,384,384]{3,2,1,0:T(8,128)(2,1)} copy(bf16[1,4,384,384]{2,3,1,0:T(8,128)(2,1)S(1)} %fusion.8) | data formatting | bytes 2359296 | tf_op jit(solution)/shard_map/convert_element_type | solution.py:40
  (1 shorter events, 0.0 us)
Async XLA Ops:
  6.5 1.4 %copy-start = (bf16[16,384,128]{2,1,0:T(8,128)(2,1)S(1)}, bf16[16,384,128]{2,1,0:T(8,128)(2,1)}, u32[]{:S(2)}) copy-start(bf16[16,384,128]{2,1,0:T(8,128)(2,1)} %param.7) | copy-start | bytes 4718596
  6.5 35.4 %copy-start.1 = (bf16[1,4,384,384]{3,2,1,0:T(8,128)(2,1)S(1)}, bf16[1,4,384,384]{3,2,1,0:T(8,128)(2,1)}, u32[]{:S(2)}) copy-start(bf16[1,4,384,384]{3,2,1,0:T(8,128)(2,1)} %param.5) | copy-start | bytes 3538948
  6.5 35.4 %all-gather.2.cloned.1.call-start = ((), (), s32[]{:S(2)}) async-start(), calls=%async_computation | async-start | bytes 1474560 | tf_op jit(solution)/shard_map/all_gather | solution.py:28
Sparse Core Ops, SparseCore 0:
  8.9 32.9 all-gather.1
where the time goes:
time: 71 us; the launch traced here: 70.7 us
  matrix products  22.2 us (31%)
  waiting for transfers between devices  17.6 us (25%)
  blocking collectives  15.3 us (22%)
  between operations  13.4 us (19%)
  local copies, waits for them, and re-layouts  2.13 us (3%)
    dot_general x4, matrix products, ladder_terms(): jnp.einsum('ac,pcb->pab', factor, halfway, preferred_element_type=jnp.flo...  18.4 us
    all_gather x1, waiting for transfers between devices, shards(): lax.all_gather(aux_factors, 'ia', axis=0, tiled=True)  16.9 us
    psum x1, blocking collectives, shards(): latent = lax.psum(partial_latent, 'ja').astype(jnp.bfloat16)  15.3 us
    dot_general x1, matrix products, shards(): jnp.einsum('iaq,jbq->ijab', latent, local_factors, preferred_element_type...  2.11 us
    dot_general x1, matrix products, shards(): jnp.einsum('ijab,jbq->iaq', doubles, local_factors, preferred_element_typ...  1.77 us
    convert_element_type x1, local copies, waits for them, and re-layouts, shards(): return (ladder + cycle_term.astype(jnp.float32)).astype(jnp.bfloat16)  1.45 us
  transfers between devices with their start and end apart: 1, of which 1 were waited for; matrix products, arithmetic and copies ran while one was open for 2% of the time, Pallas kernels for 0%

commit v1 on v0

v1 whole, which is shorter than its diff:
```python
import functools

import jax
import jax.numpy as jnp
from jax import lax
from jax.experimental import pallas as pl
from jax.experimental.pallas import tpu as pltpu
from jax.sharding import PartitionSpec as P

F32 = jnp.float32
BF16 = jnp.bfloat16
NT = (((1,), (1,)), ((), ()))
VMEM = pl.BlockSpec(memory_space=pltpu.VMEM)
HBM = pl.BlockSpec(memory_space=pltpu.HBM)


def call(kernel, outs, specs, scratch=(), aliases=None, flops=0, moved=0, name=None):
    return pl.pallas_call(
        kernel,
        out_shape=outs,
        in_specs=specs,
        out_specs=jax.tree.map(lambda o: VMEM if isinstance(o, pl.MemoryRef) else HBM, outs),
        scratch_shapes=scratch,
        input_output_aliases=aliases or {},
        cost_estimate=pl.CostEstimate(flops=flops, bytes_accessed=moved, transcendentals=0),
        compiler_params=pltpu.CompilerParams(vmem_limit_bytes=24 << 20),
        name=name,
    )


def mm(a, b):
    return jnp.dot(a, b, preferred_element_type=F32)


def mm_nt(a, b):
    return lax.dot_general(a, b, NT, preferred_element_type=F32)


def take_rows(rows, index_of, src, out, sem):
    start = pl.multiple_of(index_of() * rows, rows)
    copy = pltpu.make_async_copy(src.at[pl.ds(start, rows), :], out, sem)
    copy.start()
    copy.wait()


def latent_part(core_of, first_j, r, u_all, keep, send, u, total, sem):
    n = r.shape[0]
    copy = pltpu.make_async_copy(u_all.at[pl.ds(first_j(), n)], u, sem)
    copy.start()
    copy.wait()
    acc = mm(r[0], u[0])
    for q in range(1, n):
        acc = acc + mm(r[q], u[q])
    total[...] = acc
    half = keep.shape[0]
    core = core_of()
    keep[...] = total[pl.ds(pl.multiple_of(core * half, half), half), :]
    send[...] = total[pl.ds(pl.multiple_of((1 - core) * half, half), half), :]


def ladder_sum(r, factors, halfway):
    n, width, _ = r.shape
    rows = r[...].reshape(n * width, width)
    for p, b in enumerate(factors):
        h = mm_nt(b, rows).astype(BF16)
        for q in range(n):
            halfway[q * width : (q + 1) * width, p * width : (p + 1) * width] = h[:, q * width : (q + 1) * width]
    wide = factors[0] if len(factors) == 1 else jnp.concatenate(factors, 1)
    return mm_nt(wide, halfway[...])


def ladder_first(r, b, out, halfway):
    out[...] = ladder_sum(r, [b[...]], halfway)


def ladder_more(acc, r, b, out, halfway):
    out[...] = acc[...] + ladder_sum(r, [b[...]], halfway)


def pack(keep, got, piece, out):
    rows, width = piece.shape
    half, rank = keep.shape
    out[:rows] = piece[...]
    total = (keep[...] + got[...]).astype(BF16)
    folds = width // rank
    deep = half // folds
    for k in range(folds):
        out[rows:, k * rank : (k + 1) * rank] = total[k * deep : (k + 1) * deep]


def repack(rows, mine, theirs, out):
    out[:rows] = mine[:rows]
    out[rows : 2 * rows] = theirs[:rows]
    out[2 * rows :] = (mine[rows:].astype(F32) + theirs[rows:].astype(F32)).astype(BF16)


def place(pos, rows, mine, theirs, whole, latent):
    x, core = pos()
    for which, held in ((core, mine), (1 - core, theirs)):
        for k, half in enumerate((x, 1 - x)):
            at = pl.multiple_of((half * 2 + which) * rows, rows)
            whole[pl.ds(at, rows), :] = held[k * rows : (k + 1) * rows]
        half, rank = latent.shape[0] // 2, latent.shape[1]
        folds = whole.shape[1] // rank
        deep = half // folds
        for k in range(folds):
            at = pl.multiple_of(which * half + k * deep, deep)
            latent[pl.ds(at, deep), :] = held[2 * rows :, k * rank : (k + 1) * rank]


def ladder_packed(pos, rows, acc, r, mine, theirs, out, latent, whole, halfway):
    place(pos, rows, mine, theirs, whole, latent)
    out[...] = acc[...] + ladder_sum(r, [whole[...]], halfway)


def ladder_last(acc, r, b, latent, u, out, halfway, held, sems):
    n, width, _ = r.shape
    rows = r[...].reshape(n * width, width)
    h = mm_nt(b[...], rows).astype(BF16)
    for q in range(n):
        halfway[q * width : (q + 1) * width] = h[:, q * width : (q + 1) * width]
    copies = []
    for q in range(n):
        term = mm_nt(b[...], halfway[q * width : (q + 1) * width])
        cycle = mm_nt(latent[...], u[q]).astype(BF16)
        total = acc[:, q * width : (q + 1) * width] + term
        held[q] = (total + cycle.astype(F32)).astype(BF16)
        copies.append(pltpu.make_async_copy(held.at[q], out.at[q], sems.at[q]))
        copies[-1].start()
    for copy in copies:
        copy.wait()


def sigma_block(n_i, n_j, doubles, aux_factors, cycle_factors):
    rows_i, cols_j, width, _ = doubles.shape
    pairs = rows_i * cols_j
    rank = cycle_factors.shape[-1]
    r = doubles.reshape(pairs, width, width)
    own = aux_factors[0]
    quarter = width // 4
    flops = 2 * pairs * width * width * width

    def spot():
        j = lax.axis_index("ja")
        return lax.rem(lax.div(j, 2), 2), lax.rem(j, 2)

    def quarter_of():
        x, core = spot()
        return x * 2 + core

    core_swap = [(j, j ^ 1) for j in range(n_j)]
    chip_swap = [(j, j ^ 2) for j in range(n_j)]

    def ring(up, down):
        return [
            (i * n_j + j, (i + (down if j % 2 else up)) % n_i * n_j + j) for i in range(n_i) for j in range(n_j)
        ]

    piece = call(
        functools.partial(take_rows, quarter, quarter_of),
        pltpu.VMEM((quarter, width), BF16),
        [HBM],
        [pltpu.SemaphoreType.DMA],
        name="take",
    )(own)
    with jax.named_scope("far"):
        piece = lax.ppermute(piece, "ia", [(i, (i + n_i // 2) % n_i) for i in range(n_i)])
    near = []
    for step in range(1, n_i // 2):
        with jax.named_scope(f"near{step}"):
            near.append(lax.ppermute(own, ("ia", "ja"), ring(step, n_i - step)))

    keep, send, u = call(
        functools.partial(latent_part, lambda: spot()[1], lambda: lax.axis_index("ja") * cols_j),
        (pltpu.VMEM((width // 2, rank), F32), pltpu.VMEM((width // 2, rank), F32), pltpu.VMEM((cols_j, width, rank), BF16)),
        [VMEM, HBM],
        [pltpu.VMEM((width, rank), F32), pltpu.SemaphoreType.DMA],
        flops=2 * pairs * width * width * rank,
        moved=2 * pairs * width * width,
        name="latent_part",
    )(r, cycle_factors)
    with jax.named_scope("latent_cores"):
        got = lax.ppermute(send, "ja", core_swap)

    wide = pltpu.VMEM((width, pairs * width), F32)
    halfway = pltpu.VMEM((pairs * width, width), BF16)
    acc = call(ladder_first, wide, [VMEM] * 2, [halfway], flops=2 * flops, moved=pairs * width * width * 2, name="own")(r, own)

    fold = width // 2 * rank // width
    packed = call(pack, pltpu.VMEM((quarter + fold, width), BF16), [VMEM] * 3, name="pack")(keep, got, piece)
    with jax.named_scope("chips"):
        other = lax.ppermute(packed, "ja", chip_swap)
    packed = call(
        functools.partial(repack, quarter), pltpu.VMEM((2 * quarter + fold, width), BF16), [VMEM] * 2, name="repack"
    )(packed, other)
    apart = 4
    while apart < n_j:
        more = lax.ppermute(packed[2 * quarter :], "ja", [(j, j ^ apart) for j in range(n_j)])
        more = (packed[2 * quarter :].astype(F32) + more.astype(F32)).astype(BF16)
        packed = jnp.concatenate([packed[: 2 * quarter], more], 0)
        apart *= 2
    with jax.named_scope("cores"):
        other = lax.ppermute(packed, "ja", core_swap)
    swapped = []
    for step, factor in enumerate(near):
        with jax.named_scope(f"swap{step}"):
            swapped.append(lax.ppermute(factor, "ja", core_swap))

    acc, latent = call(
        functools.partial(ladder_packed, spot, quarter),
        (wide, pltpu.VMEM((width, rank), BF16)),
        [VMEM] * 4,
        [pltpu.VMEM((width, width), BF16), halfway],
        {0: 0},
        flops=2 * flops,
        moved=pairs * width * width * 2,
        name="far_term",
    )(acc, r, packed, other)
    for factor in near + swapped[:-1]:
        acc = call(
            ladder_more, wide, [VMEM] * 3, [halfway], {0: 0}, flops=2 * flops, moved=pairs * width * width * 2, name="term"
        )(acc, r, factor)
    out = call(
        ladder_last,
        jax.ShapeDtypeStruct((pairs, width, width), BF16),
        [VMEM] * 5,
        [halfway, pltpu.VMEM((pairs, width, width), BF16), pltpu.SemaphoreType.DMA((pairs,))],
        flops=2 * flops,
        moved=pairs * width * width * 2,
        name="last",
    )(acc, r, swapped[-1], latent, u)
    return out.reshape(doubles.shape)


def solution(mesh):
    n_i, n_j = mesh.shape["ia"], mesh.shape["ja"]
    in_specs = (P(("grp", "ia"), "ja", None, None), P("ia", None, None), P())
    out_specs = P(("grp", "ia"), "ja", None, None)
    block = functools.partial(sigma_block, n_i, n_j)
    return jax.shard_map(block, mesh=mesh, in_specs=in_specs, out_specs=out_specs, check_vma=False)
```

time: 71 us -> 28.7 us (0.40)
  matrix products: 22.2 us -> 0 us
  blocking collectives: 15.3 us -> 0 us
  between operations: 13.4 us -> 0.09 us
  starting transfers between devices: 0.01 us -> 8.07 us
  Pallas kernels: 0 us -> 7.75 us
  waiting for transfers between devices: 17.6 us -> 9.98 us
    dot_general x6 -> x0, matrix products: 22.2 us -> none  [the longest x4 18.4 us: ladder_terms(): jnp.einsum('ac,pcb->pab', factor, halfway, preferred_element_type=jnp.flo...]
    all_gather x1 -> x0, waiting for transfers between devices: 16.9 us -> none  [shards(): lax.all_gather(aux_factors, 'ia', axis=0, tiled=True)]
    psum x1 -> x0, blocking collectives: 15.3 us -> none  [shards(): latent = lax.psum(partial_latent, 'ja').astype(jnp.bfloat16)]
    ppermute x0 -> x6, waiting for transfers between devices: none -> 9.98 us  [the longest x1 6.19 us: sigma_block(): lax.ppermute(piece, 'ia', [(i, (i + n_i // 2) % n_i) for i in range(n_i)])]
    ppermute x0 -> x6, starting transfers between devices: none -> 8.07 us  [the longest x1 3.05 us: sigma_block(): near.append(lax.ppermute(own, ('ia', 'ja'), ring(step, n_i - step)))]
    pallas_call x0 -> x8, Pallas kernels: none -> 7.75 us  [the longest x1 2.65 us: sigma_block(): call(ladder_last, jax.ShapeDtypeStruct((pairs, width, width), BF16), [VME...]
    unnamed x4 -> x8, local copies, waits for them, and re-layouts: 0.67 us -> 2.68 us
    convert_element_type x1 -> x0, local copies, waits for them, and re-layouts: 1.45 us -> none  [shards(): return (ladder + cycle_term.astype(jnp.float32)).astype(jnp.bfloat16)]
  transfers between devices with their start and end apart: 1 -> 6, of which waited for: 1 -> 2; matrix products, arithmetic and copies ran while one was open for 2% -> 0% of each run, Pallas kernels for 0% -> 18%
where the time goes in v1:
time: 28.7 us; the launch traced here: 28.6 us
  waiting for transfers between devices  9.98 us (35%)
  starting transfers between devices  8.07 us (28%)
  Pallas kernels  7.75 us (27%)
  local copies, waits for them, and re-layouts  2.68 us (9%)
    ppermute x1, waiting for transfers between devices, sigma_block(): lax.ppermute(piece, 'ia', [(i, (i + n_i // 2) % n_i) for i in range(n_i)])  6.19 us
    ppermute x1, waiting for transfers between devices, sigma_block(): other = lax.ppermute(packed, 'ja', chip_swap)  3.77 us
    ppermute x1, starting transfers between devices, sigma_block(): near.append(lax.ppermute(own, ('ia', 'ja'), ring(step, n_i - step)))  3.05 us
    unnamed x8, local copies, waits for them, and re-layouts  2.68 us
    pallas_call x1, Pallas kernels, sigma_block(): call(ladder_last, jax.ShapeDtypeStruct((pairs, width, width), BF16), [VME...  2.65 us
    ppermute x1, starting transfers between devices, sigma_block(): got = lax.ppermute(send, 'ja', core_swap)  1.65 us
    ppermute x1, starting transfers between devices, sigma_block(): other = lax.ppermute(packed, 'ja', chip_swap)  1.56 us
    pallas_call x1, Pallas kernels, sigma_block(): call(functools.partial(ladder_packed, spot, quarter), (wide, pltpu.VMEM((...  1.44 us
  transfers between devices with their start and end apart: 6, of which 2 were waited for; matrix products, arithmetic and copies ran while one was open for 0% of the time, Pallas kernels for 18%

profile of v1, /device:TPU:0, one launch (start us, length us, event | category | flops | bytes accessed | tf_op | source)
XLA Modules:
  0.0 28.6 jit_solution(9110150732763577251)
XLA Ops:
  0.0 3.1 %collective-permute-start.4 = (bf16[384,384]{1,0:T(8,128)(2,1)}, bf16[384,384]{1,0:T(8,128)(2,1)S(1)}, u32[]{:S(2)}, u32[]{:S(2)}) collective-permute-start(bf16[384,384]{1,0:T(8,128)(2,1)} %bitcast.8), channel_id=1, source_target_pairs={{0,4},{1,13},{2,6},{3,15},{4,8},{5,1},{6,10},{7,3},{8,12},{9,5},{1... | collective-permute-start | bytes 884744 | tf_op jit(solution)/shard_map/near1/ppermute | solution.py:171
  3.1 0.0 copy-start
  3.1 1.3 %copy-done = bf16[1,4,384,384]{3,2,1,0:T(8,128)(2,1)S(1)} copy-done((bf16[1,4,384,384]{3,2,1,0:T(8,128)(2,1)S(1)}, bf16[1,4,384,384]{3,2,1,0:T(8,128)(2,1)}, u32[]{:S(2)}) %copy-start) | copy-done | bytes 1179672
  4.3 0.0 copy-start.2
  4.3 1.4 %copy-done.2 = bf16[16,384,128]{2,1,0:T(8,128)(2,1)S(1)} copy-done((bf16[16,384,128]{2,1,0:T(8,128)(2,1)S(1)}, bf16[16,384,128]{2,1,0:T(8,128)(2,1)}, u32[]{:S(2)}) %copy-start.2) | copy-done | bytes 1572888
  5.7 0.0 copy-start.3
  5.7 0.0 copy-start.1
  5.7 0.7 %latent_part.1 = (f32[192,128]{1,0:T(8,128)S(1)}, f32[192,128]{1,0:T(8,128)S(1)}, bf16[4,384,128]{2,1,0:T(8,128)(2,1)S(1)}) custom-call(bf16[4,384,384]{2,1,0:T(8,128)(2,1)S(1)} %bitcast.3, bf16[16,384,128]{2,1,0:T(8,128)(2,1)S(1)} %copy-done.2), custom_call_target="tpu_custom_call" | custom-call | flops 150994944 | bytes 1179648 | tf_op jit(solution)/shard_map/latent_part/pallas_call | solution.py:173
  6.4 1.7 %collective-permute-start = (f32[192,128]{1,0:T(8,128)S(1)}, f32[192,128]{1,0:T(8,128)S(1)}, u32[]{:S(2)}, u32[]{:S(2)}) collective-permute-start(f32[192,128]{1,0:T(8,128)S(1)} %get-tuple-element.11), channel_id=1, source_target_pairs={{0,1},{1,0},{2,3},{3,2},{4,5},{5,4},{6,7},{7,6},{8,9},{9,8},{10,11... | collective-permute-start | bytes 294920 | tf_op jit(solution)/shard_map/latent_cores/ppermute | solution.py:183
  8.1 0.0 copy-done.3
  8.1 0.1 take.1
  8.2 1.2 %collective-permute-start.1 = (bf16[96,384]{1,0:T(8,128)(2,1)S(1)}, bf16[96,384]{1,0:T(8,128)(2,1)S(1)}, u32[]{:S(2)}, u32[]{:S(2)}) collective-permute-start(bf16[96,384]{1,0:T(8,128)(2,1)S(1)} %take.1), channel_id=1, source_target_pairs={{0,8},{4,12},{8,0},{12,4},{1,9},{5,13},{9,1},{13,5},{2,10},{6,14},... | collective-permute-start | bytes 221192 | tf_op jit(solution)/shard_map/far/ppermute | solution.py:167
  9.4 6.2 %collective-permute-done.1.piece = bf16[96,384]{1,0:T(8,128)(2,1)S(1)} collective-permute-done((bf16[96,384]{1,0:T(8,128)(2,1)S(1)}, bf16[96,384]{1,0:T(8,128)(2,1)S(1)}, u32[]{:S(2)}, u32[]{:S(2)}) %collective-permute-start.1) | collective-permute-done | bytes 73760 | tf_op jit(solution)/shard_map/far/ppermute | solution.py:167
  15.6 0.0 collective-permute-done.got
  15.6 1.6 %collective-permute-start.2 = (bf16[160,384]{1,0:T(8,128)(2,1)S(1)}, bf16[160,384]{1,0:T(8,128)(2,1)S(1)}, u32[]{:S(2)}, u32[]{:S(2)}) collective-permute-start(bf16[160,384]{1,0:T(8,128)(2,1)S(1)} %pack.1.mine), channel_id=1, source_target_pairs={{0,2},{1,3},{2,0},{3,1},{4,6},{5,7},{6,4},{7,5},{8,10},{9,11},{10,... | collective-permute-start | bytes 368648 | tf_op jit(solution)/shard_map/chips/ppermute | solution.py:192
  17.2 3.8 %collective-permute-done.2.theirs = bf16[160,384]{1,0:T(8,128)(2,1)S(1)} collective-permute-done((bf16[160,384]{1,0:T(8,128)(2,1)S(1)}, bf16[160,384]{1,0:T(8,128)(2,1)S(1)}, u32[]{:S(2)}, u32[]{:S(2)}) %collective-permute-start.2) | collective-permute-done | bytes 122912 | tf_op jit(solution)/shard_map/chips/ppermute | solution.py:192
  21.0 0.1 collective-permute-start.3
  21.1 0.0 collective-permute-done.4.b
  21.1 0.5 %collective-permute-start.5 = (bf16[384,384]{1,0:T(8,128)(2,1)S(1)}, bf16[384,384]{1,0:T(8,128)(2,1)S(1)}, u32[]{:S(2)}, u32[]{:S(2)}) collective-permute-start(bf16[384,384]{1,0:T(8,128)(2,1)S(1)} %collective-permute-done.4.b), channel_id=1, source_target_pairs={{0,1},{1,0},{2,3},{3,2},{4,5},{5,4},{6,7},{7,6},{8,9},{9,8},{10,11... | collective-permute-start | bytes 884744 | tf_op jit(solution)/shard_map/swap0/ppermute | solution.py:207
  21.6 0.0 copy-done.1
  21.6 1.4 %own.1.acc = f32[384,1536]{1,0:T(8,128)S(1)} custom-call(bf16[4,384,384]{2,1,0:T(8,128)(2,1)S(1)} %bitcast.4, bf16[384,384]{1,0:T(8,128)(2,1)S(1)} %bitcast.10), custom_call_target="tpu_custom_call" | custom-call | flops 905969664 | bytes 1179648 | tf_op jit(solution)/shard_map/own/pallas_call | solution.py:187
  23.0 0.0 collective-permute-done.3.theirs
  23.0 1.4 %far_term.1 = (f32[384,1536]{1,0:T(8,128)S(1)}, bf16[384,128]{1,0:T(8,128)(2,1)S(1)}) custom-call(f32[384,1536]{1,0:T(8,128)S(1)} %own.1.acc, bf16[4,384,384]{2,1,0:T(8,128)(2,1)S(1)} %bitcast.5, bf16[256,384]{1,0:T(8,128)(2,1)S(1)} %repack.1.mine, bf16[256,384]{1,0:T(8,128)(2,1)S(1)} %collective-permute-done.3.theirs), custom_call_target="tpu_custom_call", output_to_operand_aliasing={{0}: (0, {})} | custom-call | flops 905969664 | bytes 1179648 | tf_op jit(solution)/shard_map/far_term/pallas_call | solution.py:209
  24.5 1.4 %term.1.acc = f32[384,1536]{1,0:T(8,128)S(1)} custom-call(f32[384,1536]{1,0:T(8,128)S(1)} %get-tuple-element.12.acc, bf16[4,384,384]{2,1,0:T(8,128)(2,1)S(1)} %bitcast.6, bf16[384,384]{1,0:T(8,128)(2,1)S(1)} %collective-permute-done.4.b), custom_call_target="tpu_custom_call", output_to_operand_aliasing={{}: (0, {})} | custom-call | flops 905969664 | bytes 1179648 | tf_op jit(solution)/shard_map/term/pallas_call | solution.py:220
  25.9 0.0 collective-permute-done.5.b
  25.9 2.7 %last.1 = bf16[4,384,384]{2,1,0:T(8,128)(2,1)} custom-call(f32[384,1536]{1,0:T(8,128)S(1)} %term.1.acc, bf16[4,384,384]{2,1,0:T(8,128)(2,1)S(1)} %bitcast.7, bf16[384,384]{1,0:T(8,128)(2,1)S(1)} %collective-permute-done.5.b, bf16[384,128]{1,0:T(8,128)(2,1)S(1)} %get-tuple-element.13.latent, bf16[4,384,128]{2,1,0:T(8,128)(2,1)S(1)} %get-tuple-element.14.u), custom_call_target="tpu_custom_call" | custom-call | flops 905969664 | bytes 1179648 | tf_op jit(solution)/shard_map/last/pallas_call | solution.py:223
  (2 shorter events, 0.0 us)
Async XLA Ops:
  0.0 21.1 %collective-permute-start.4 = (bf16[384,384]{1,0:T(8,128)(2,1)}, bf16[384,384]{1,0:T(8,128)(2,1)S(1)}, u32[]{:S(2)}, u32[]{:S(2)}) collective-permute-start(bf16[384,384]{1,0:T(8,128)(2,1)} %bitcast.8), channel_id=1, source_target_pairs={{0,4},{1,13},{2,6},{3,15},{4,8},{5,1},{6,10},{7,3},{8,12},{9,5},{1... | collective-permute-start | bytes 884744 | tf_op jit(solution)/shard_map/near1/ppermute | solution.py:171
  3.1 1.3 %copy-start = (bf16[1,4,384,384]{3,2,1,0:T(8,128)(2,1)S(1)}, bf16[1,4,384,384]{3,2,1,0:T(8,128)(2,1)}, u32[]{:S(2)}) copy-start(bf16[1,4,384,384]{3,2,1,0:T(8,128)(2,1)} %param.3) | copy-start | bytes 3538948
  4.3 1.4 %copy-start.2 = (bf16[16,384,128]{2,1,0:T(8,128)(2,1)S(1)}, bf16[16,384,128]{2,1,0:T(8,128)(2,1)}, u32[]{:S(2)}) copy-start(bf16[16,384,128]{2,1,0:T(8,128)(2,1)} %u_all.1) | copy-start | bytes 4718596
  5.7 2.4 %copy-start.3 = (bf16[1,384,384]{2,1,0:T(8,128)(2,1)S(1)}, bf16[1,384,384]{2,1,0:T(8,128)(2,1)}, u32[]{:S(2)}) copy-start(bf16[1,384,384]{2,1,0:T(8,128)(2,1)} %param.4) | copy-start | bytes 884740
  5.7 15.9 %copy-start.1 = (bf16[1,4,384,384]{3,2,1,0:T(8,128)(2,1)S(1)}, bf16[1,4,384,384]{3,2,1,0:T(8,128)(2,1)}, u32[]{:S(2)}) copy-start(bf16[1,4,384,384]{3,2,1,0:T(8,128)(2,1)} %param.3) | copy-start | bytes 3538948
  6.4 9.2 %collective-permute-start = (f32[192,128]{1,0:T(8,128)S(1)}, f32[192,128]{1,0:T(8,128)S(1)}, u32[]{:S(2)}, u32[]{:S(2)}) collective-permute-start(f32[192,128]{1,0:T(8,128)S(1)} %get-tuple-element.11), channel_id=1, source_target_pairs={{0,1},{1,0},{2,3},{3,2},{4,5},{5,4},{6,7},{7,6},{8,9},{9,8},{10,11... | collective-permute-start | bytes 294920 | tf_op jit(solution)/shard_map/latent_cores/ppermute | solution.py:183
  8.2 7.4 %collective-permute-start.1 = (bf16[96,384]{1,0:T(8,128)(2,1)S(1)}, bf16[96,384]{1,0:T(8,128)(2,1)S(1)}, u32[]{:S(2)}, u32[]{:S(2)}) collective-permute-start(bf16[96,384]{1,0:T(8,128)(2,1)S(1)} %take.1), channel_id=1, source_target_pairs={{0,8},{4,12},{8,0},{12,4},{1,9},{5,13},{9,1},{13,5},{2,10},{6,14},... | collective-permute-start | bytes 221192 | tf_op jit(solution)/shard_map/far/ppermute | solution.py:167
  15.6 5.3 %collective-permute-start.2 = (bf16[160,384]{1,0:T(8,128)(2,1)S(1)}, bf16[160,384]{1,0:T(8,128)(2,1)S(1)}, u32[]{:S(2)}, u32[]{:S(2)}) collective-permute-start(bf16[160,384]{1,0:T(8,128)(2,1)S(1)} %pack.1.mine), channel_id=1, source_target_pairs={{0,2},{1,3},{2,0},{3,1},{4,6},{5,7},{6,4},{7,5},{8,10},{9,11},{10,... | collective-permute-start | bytes 368648 | tf_op jit(solution)/shard_map/chips/ppermute | solution.py:192
  21.0 2.0 %collective-permute-start.3 = (bf16[256,384]{1,0:T(8,128)(2,1)S(1)}, bf16[256,384]{1,0:T(8,128)(2,1)S(1)}, u32[]{:S(2)}, u32[]{:S(2)}) collective-permute-start(bf16[256,384]{1,0:T(8,128)(2,1)S(1)} %repack.1.mine), channel_id=1, source_target_pairs={{0,1},{1,0},{2,3},{3,2},{4,5},{5,4},{6,7},{7,6},{8,9},{9,8},{10,11... | collective-permute-start | bytes 589832 | tf_op jit(solution)/shard_map/cores/ppermute | solution.py:203
  21.1 4.8 %collective-permute-start.5 = (bf16[384,384]{1,0:T(8,128)(2,1)S(1)}, bf16[384,384]{1,0:T(8,128)(2,1)S(1)}, u32[]{:S(2)}, u32[]{:S(2)}) collective-permute-start(bf16[384,384]{1,0:T(8,128)(2,1)S(1)} %collective-permute-done.4.b), channel_id=1, source_target_pairs={{0,1},{1,0},{2,3},{3,2},{4,5},{5,4},{6,7},{7,6},{8,9},{9,8},{10,11... | collective-permute-start | bytes 884744 | tf_op jit(solution)/shard_map/swap0/ppermute | solution.py:207

commit v2 on v1

v2 whole, which is shorter than its diff:
```python
import functools

import jax
import jax.numpy as jnp
from jax import lax
from jax.experimental import pallas as pl
from jax.experimental.pallas import tpu as pltpu
from jax.sharding import PartitionSpec as P

F32 = jnp.float32
BF16 = jnp.bfloat16
NT = (((1,), (1,)), ((), ()))
VMEM = pl.BlockSpec(memory_space=pltpu.VMEM)
HBM = pl.BlockSpec(memory_space=pltpu.HBM)


def call(kernel, outs, specs, scratch=(), aliases=None, flops=0, moved=0):
    return pl.pallas_call(
        kernel,
        out_shape=outs,
        in_specs=specs,
        out_specs=jax.tree.map(lambda o: VMEM if isinstance(o, pl.MemoryRef) else HBM, outs),
        scratch_shapes=scratch,
        input_output_aliases=aliases or {},
        cost_estimate=pl.CostEstimate(flops=flops, bytes_accessed=moved, transcendentals=0),
        compiler_params=pltpu.CompilerParams(vmem_limit_bytes=24 << 20),
    )


def in_hbm(x):
    return pltpu.with_memory_space_constraint(x, pltpu.HBM)


def mm(a, b):
    return jnp.dot(a, b, preferred_element_type=F32)


def mm_nt(a, b):
    return lax.dot_general(a, b, NT, preferred_element_type=F32)


def take_rows(rows, index_of, src, out, sem):
    start = pl.multiple_of(index_of() * rows, rows)
    copy = pltpu.make_async_copy(src.at[pl.ds(start, rows), :], out, sem)
    copy.start()
    copy.wait()


def latent_part(core_of, first_j, r_src, own_src, u_src, keep, send, r, own, u, total, sems):
    n = r.shape[0]
    copies = [pltpu.make_async_copy(u_src.at[pl.ds(first_j(), n)], u, sems.at[n])]
    copies += [pltpu.make_async_copy(r_src.at[q], r.at[q], sems.at[q]) for q in range(n)]
    copies += [pltpu.make_async_copy(own_src, own, sems.at[n + 1])]
    for copy in copies:
        copy.start()
    copies[0].wait()
    for q in range(n):
        copies[1 + q].wait()
        part = mm(r[q], u[q])
        total[...] = part if q == 0 else total[...] + part
    half = keep.shape[0]
    core = core_of()
    keep[...] = total[pl.ds(pl.multiple_of(core * half, half), half), :]
    send[...] = total[pl.ds(pl.multiple_of((1 - core) * half, half), half), :]
    copies[-1].wait()


def ladder_sum(r, factors, halfway):
    n, width, _ = r.shape
    rows = r[...].reshape(n * width, width)
    for p, b in enumerate(factors):
        h = mm_nt(b, rows).astype(BF16)
        for q in range(n):
            halfway[q * width : (q + 1) * width, p * width : (p + 1) * width] = h[:, q * width : (q + 1) * width]
    wide = factors[0] if len(factors) == 1 else jnp.concatenate(factors, 1)
    return mm_nt(wide, halfway[...])


def ladder_first(r, b, out, halfway):
    out[...] = ladder_sum(r, [b[...]], halfway)


def ladder_more(acc, r, b, out, halfway):
    out[...] = acc[...] + ladder_sum(r, [b[...]], halfway)


def pack(keep, got, piece, out):
    rows, width = piece.shape
    half, rank = keep.shape
    out[:rows] = piece[...]
    total = (keep[...] + got[...]).astype(BF16)
    folds = width // rank
    deep = half // folds
    for k in range(folds):
        out[rows:, k * rank : (k + 1) * rank] = total[k * deep : (k + 1) * deep]


def repack(rows, mine, theirs, out):
    out[:rows] = mine[:rows]
    out[rows : 2 * rows] = theirs[:rows]
    out[2 * rows :] = (mine[rows:].astype(F32) + theirs[rows:].astype(F32)).astype(BF16)


def place(pos, rows, mine, theirs, whole, latent):
    x, core = pos()
    for which, held in ((core, mine), (1 - core, theirs)):
        for k, half in enumerate((x, 1 - x)):
            at = pl.multiple_of((half * 2 + which) * rows, rows)
            whole[pl.ds(at, rows), :] = held[k * rows : (k + 1) * rows]
        half, rank = latent.shape[0] // 2, latent.shape[1]
        folds = whole.shape[1] // rank
        deep = half // folds
        for k in range(folds):
            at = pl.multiple_of(which * half + k * deep, deep)
            latent[pl.ds(at, deep), :] = held[2 * rows :, k * rank : (k + 1) * rank]


def ladder_last(pos, rows, acc, r, mine, theirs, u, out, whole, latent, halfway, held, sems):
    n, width, _ = r.shape
    place(pos, rows, mine, theirs, whole, latent)
    b = whole[...]
    h = mm_nt(b, r[...].reshape(n * width, width)).astype(BF16)
    for q in range(n):
        halfway[q * width : (q + 1) * width] = h[:, q * width : (q + 1) * width]
    copies = []
    for q in range(n):
        term = mm_nt(b, halfway[q * width : (q + 1) * width])
        cycle = mm_nt(latent[...], u[q]).astype(BF16)
        total = acc[:, q * width : (q + 1) * width] + term
        held[q] = (total + cycle.astype(F32)).astype(BF16)
        copies.append(pltpu.make_async_copy(held.at[q], out.at[q], sems.at[q]))
        copies[-1].start()
    for copy in copies:
        copy.wait()


def sigma_block(n_i, n_j, doubles, aux_factors, cycle_factors):
    rows_i, cols_j, width, _ = doubles.shape
    pairs = rows_i * cols_j
    rank = cycle_factors.shape[-1]
    r = doubles.reshape(pairs, width, width)
    own = aux_factors.reshape(width, width)
    quarter = width // 4
    flops = 2 * pairs * width * width * width

    def spot():
        j = lax.axis_index("ja")
        return lax.rem(lax.div(j, 2), 2), lax.rem(j, 2)

    def quarter_of():
        x, core = spot()
        return x * 2 + core

    core_swap = [(j, j ^ 1) for j in range(n_j)]
    chip_swap = [(j, j ^ 2) for j in range(n_j)]

    def ring(up, down):
        return [
            (i * n_j + j, (i + (down if j % 2 else up)) % n_i * n_j + j) for i in range(n_i) for j in range(n_j)
        ]

    piece = call(
        functools.partial(take_rows, quarter, quarter_of),
        pltpu.VMEM((quarter, width), BF16),
        [HBM],
        [pltpu.SemaphoreType.DMA],
    )(in_hbm(own))
    piece = lax.ppermute(piece, "ia", [(i, (i + n_i // 2) % n_i) for i in range(n_i)])
    near = []
    for step in range(1, n_i // 2):
        near.append(lax.ppermute(own, ("ia", "ja"), ring(step, n_i - step)))

    keep, send, r, own, u = call(
        functools.partial(latent_part, lambda: spot()[1], lambda: lax.axis_index("ja") * cols_j),
        (
            pltpu.VMEM((width // 2, rank), F32),
            pltpu.VMEM((width // 2, rank), F32),
            pltpu.VMEM((pairs, width, width), BF16),
            pltpu.VMEM((width, width), BF16),
            pltpu.VMEM((cols_j, width, rank), BF16),
        ),
        [HBM] * 3,
        [pltpu.VMEM((width, rank), F32), pltpu.SemaphoreType.DMA((pairs + 2,))],
        flops=2 * pairs * width * width * rank,
        moved=2 * pairs * width * width,
    )(in_hbm(r), in_hbm(own), in_hbm(cycle_factors))
    got = lax.ppermute(send, "ja", core_swap)

    wide = pltpu.VMEM((width, pairs * width), F32)
    halfway = pltpu.VMEM((pairs * width, width), BF16)
    acc = call(ladder_first, wide, [VMEM] * 2, [halfway], flops=2 * flops, moved=pairs * width * width * 2)(r, own)

    fold = width // 2 * rank // width
    packed = call(pack, pltpu.VMEM((quarter + fold, width), BF16), [VMEM] * 3)(keep, got, piece)
    other = lax.ppermute(packed, "ja", chip_swap)
    packed = call(
        functools.partial(repack, quarter), pltpu.VMEM((2 * quarter + fold, width), BF16), [VMEM] * 2
    )(packed, other)
    apart = 4
    while apart < n_j:
        more = lax.ppermute(packed[2 * quarter :], "ja", [(j, j ^ apart) for j in range(n_j)])
        more = (packed[2 * quarter :].astype(F32) + more.astype(F32)).astype(BF16)
        packed = jnp.concatenate([packed[: 2 * quarter], more], 0)
        apart *= 2
    other = lax.ppermute(packed, "ja", core_swap)
    swapped = []
    for factor in near:
        swapped.append(lax.ppermute(factor, "ja", core_swap))

    for factors in (near, swapped):
        for factor in factors:
            acc = call(
                ladder_more, wide, [VMEM] * 3, [halfway], {0: 0}, flops=2 * flops, moved=pairs * width * width * 2
            )(acc, r, factor)
    out = call(
        functools.partial(ladder_last, spot, quarter),
        jax.ShapeDtypeStruct((pairs, width, width), BF16),
        [VMEM] * 5,
        [
            pltpu.VMEM((width, width), BF16),
            pltpu.VMEM((width, rank), BF16),
            halfway,
            pltpu.VMEM((pairs, width, width), BF16),
            pltpu.SemaphoreType.DMA((pairs,)),
        ],
        flops=2 * flops,
        moved=pairs * width * width * 2,
    )(acc, r, packed, other, u)
    return out.reshape(doubles.shape)


def solution(mesh):
    n_i, n_j = mesh.shape["ia"], mesh.shape["ja"]
    in_specs = (P(("grp", "ia"), "ja", None, None), P("ia", None, None), P())
    out_specs = P(("grp", "ia"), "ja", None, None)

    def block(*args):
        return sigma_block(n_i, n_j, *args)

    return jax.shard_map(block, mesh=mesh, in_specs=in_specs, out_specs=out_specs, check_vma=False)
```

time: 28.7 us -> 27.8 us (0.969)
  local copies, waits for them, and re-layouts: 2.68 us -> 0 us
  Pallas kernels: 7.75 us -> 10.1 us
  starting transfers between devices: 8.07 us -> 7.55 us
    ppermute x1, waiting for transfers between devices: 0.01 us -> 4.32 us  [sigma_block(): near.append(lax.ppermute(own, ('ia', 'ja'), ring(step, n_i - step)))]
    ppermute x1, waiting for transfers between devices: 6.19 us -> 2.19 us  [sigma_block(): lax.ppermute(piece, 'ia', [(i, (i + n_i // 2) % n_i) for i in range(n_i)])]
    unnamed x8 -> x0, local copies, waits for them, and re-layouts: 2.68 us -> none
    pallas_call x1, Pallas kernels: 0.69 us -> 2.2 us  [sigma_block(): call(functools.partial(latent_part, lambda: spot()[1], lambda: lax.axis_i...]
    pallas_call x3 -> x2, Pallas kernels: 4.11 us -> 2.66 us  [the longest x1 2.65 us: sigma_block(): call(functools.partial(ladder_last, spot, quarter), jax.ShapeDtypeStruct(...]
    pallas_call x1 -> x2, Pallas kernels: 1.43 us -> 2.86 us  [sigma_block(): call(ladder_more, wide, [VMEM] * 3, [halfway], {0: 0}, flops=2 * flops, m...]
    pallas_call x1, Pallas kernels: 0.08 us -> 0.89 us  [sigma_block(): call(functools.partial(take_rows, quarter, quarter_of), pltpu.VMEM((quart...]
    ppermute x1, starting transfers between devices: 0.49 us -> 0.01 us  [sigma_block(): swapped.append(lax.ppermute(factor, 'ja', core_swap))]
  transfers between devices with their start and end apart: 6 -> 6, of which waited for: 2 -> 3; matrix products, arithmetic and copies ran while one was open for 0% -> 0% of each run, Pallas kernels for 18% -> 27%
where the time goes in v2:
time: 27.8 us; the launch traced here: 27.7 us
  Pallas kernels  10.1 us (36%)
  waiting for transfers between devices  9.97 us (36%)
  starting transfers between devices  7.55 us (27%)
    ppermute x1, waiting for transfers between devices, sigma_block(): near.append(lax.ppermute(own, ('ia', 'ja'), ring(step, n_i - step)))  4.32 us
    ppermute x1, waiting for transfers between devices, sigma_block(): other = lax.ppermute(packed, 'ja', chip_swap)  3.46 us
    ppermute x1, starting transfers between devices, sigma_block(): near.append(lax.ppermute(own, ('ia', 'ja'), ring(step, n_i - step)))  3.05 us
    pallas_call x2, Pallas kernels, sigma_block(): call(ladder_more, wide, [VMEM] * 3, [halfway], {0: 0}, flops=2 * flops, m...  2.86 us
    pallas_call x1, Pallas kernels, sigma_block(): call(functools.partial(ladder_last, spot, quarter), jax.ShapeDtypeStruct(...  2.65 us
    pallas_call x1, Pallas kernels, sigma_block(): call(functools.partial(latent_part, lambda: spot()[1], lambda: lax.axis_i...  2.2 us
    ppermute x1, waiting for transfers between devices, sigma_block(): lax.ppermute(piece, 'ia', [(i, (i + n_i // 2) % n_i) for i in range(n_i)])  2.19 us
    ppermute x1, starting transfers between devices, sigma_block(): other = lax.ppermute(packed, 'ja', chip_swap)  1.67 us
  transfers between devices with their start and end apart: 6, of which 3 were waited for; matrix products, arithmetic and copies ran while one was open for 0% of the time, Pallas kernels for 27%

profile of v2, /device:TPU:0, one launch (start us, length us, event | category | flops | bytes accessed | tf_op | source)
XLA Modules:
  0.0 27.7 jit_solution(10354414551923844829)
XLA Ops:
  0.0 3.1 %collective-permute-start = (bf16[384,384]{1,0:T(8,128)(2,1)}, bf16[384,384]{1,0:T(8,128)(2,1)S(1)}, u32[]{:S(2)}, u32[]{:S(2)}) collective-permute-start(bf16[384,384]{1,0:T(8,128)(2,1)} %bitcast.3), channel_id=1, source_target_pairs={{0,4},{1,13},{2,6},{3,15},{4,8},{5,1},{6,10},{7,3},{8,12},{9,5},{1... | collective-permute-start | bytes 884744 | tf_op jit(solution)/shard_map/ppermute | solution.py:171
  3.1 2.2 %shard_map.37 = (f32[192,128]{1,0:T(8,128)S(1)}, f32[192,128]{1,0:T(8,128)S(1)}, bf16[4,384,384]{2,1,0:T(8,128)(2,1)S(1)}, bf16[384,384]{1,0:T(8,128)(2,1)S(1)}, bf16[4,384,128]{2,1,0:T(8,128)(2,1)S(1)}) custom-call(bf16[4,384,384]{2,1,0:T(8,128)(2,1)} %bitcast.6, bf16[384,384]{1,0:T(8,128)(2,1)} %bitcast.4, bf16[16,384,128]{2,1,0:T(8,128)(2,1)} %u_src.1), custom_call_target="tpu_custom_call" | custom-call | flops 150994944 | bytes 1179648 | tf_op jit(solution)/shard_map/pallas_call | solution.py:173
  5.3 1.6 %collective-permute-start.2 = (f32[192,128]{1,0:T(8,128)S(1)}, f32[192,128]{1,0:T(8,128)S(1)}, u32[]{:S(2)}, u32[]{:S(2)}) collective-permute-start(f32[192,128]{1,0:T(8,128)S(1)} %get-tuple-element.13), channel_id=1, source_target_pairs={{0,1},{1,0},{2,3},{3,2},{4,5},{5,4},{6,7},{7,6},{8,9},{9,8},{10,11... | collective-permute-start | bytes 294920 | tf_op jit(solution)/shard_map/ppermute | solution.py:187
  6.9 0.9 %shard_map.41 = bf16[96,384]{1,0:T(8,128)(2,1)S(1)} custom-call(bf16[384,384]{1,0:T(8,128)(2,1)} %bitcast.5), custom_call_target="tpu_custom_call" | custom-call | tf_op jit(solution)/shard_map/pallas_call | solution.py:162
  7.8 1.1 %collective-permute-start.3 = (bf16[96,384]{1,0:T(8,128)(2,1)S(1)}, bf16[96,384]{1,0:T(8,128)(2,1)S(1)}, u32[]{:S(2)}, u32[]{:S(2)}) collective-permute-start(bf16[96,384]{1,0:T(8,128)(2,1)S(1)} %shard_map.41), channel_id=1, source_target_pairs={{0,8},{4,12},{8,0},{12,4},{1,9},{5,13},{9,1},{13,5},{2,10},{6,14},... | collective-permute-start | bytes 221192 | tf_op jit(solution)/shard_map/ppermute | solution.py:168
  8.9 4.3 %collective-permute-done.b = bf16[384,384]{1,0:T(8,128)(2,1)S(1)} collective-permute-done((bf16[384,384]{1,0:T(8,128)(2,1)}, bf16[384,384]{1,0:T(8,128)(2,1)S(1)}, u32[]{:S(2)}, u32[]{:S(2)}) %collective-permute-start) | collective-permute-done | bytes 294944 | tf_op jit(solution)/shard_map/ppermute | solution.py:171
  13.2 0.0 collective-permute-start.1
  13.2 2.2 %collective-permute-done.3.piece = bf16[96,384]{1,0:T(8,128)(2,1)S(1)} collective-permute-done((bf16[96,384]{1,0:T(8,128)(2,1)S(1)}, bf16[96,384]{1,0:T(8,128)(2,1)S(1)}, u32[]{:S(2)}, u32[]{:S(2)}) %collective-permute-start.3) | collective-permute-done | bytes 73760 | tf_op jit(solution)/shard_map/ppermute | solution.py:168
  15.4 0.0 collective-permute-done.2.got
  15.5 1.7 %collective-permute-start.4 = (bf16[160,384]{1,0:T(8,128)(2,1)S(1)}, bf16[160,384]{1,0:T(8,128)(2,1)S(1)}, u32[]{:S(2)}, u32[]{:S(2)}) collective-permute-start(bf16[160,384]{1,0:T(8,128)(2,1)S(1)} %shard_map.42.mine), channel_id=1, source_target_pairs={{0,2},{1,3},{2,0},{3,1},{4,6},{5,7},{6,4},{7,5},{8,10},{9,11},{10,... | collective-permute-start | bytes 368648 | tf_op jit(solution)/shard_map/ppermute | solution.py:195
  17.1 3.5 %collective-permute-done.4.theirs = bf16[160,384]{1,0:T(8,128)(2,1)S(1)} collective-permute-done((bf16[160,384]{1,0:T(8,128)(2,1)S(1)}, bf16[160,384]{1,0:T(8,128)(2,1)S(1)}, u32[]{:S(2)}, u32[]{:S(2)}) %collective-permute-start.4) | collective-permute-done | bytes 122912 | tf_op jit(solution)/shard_map/ppermute | solution.py:195
  20.6 0.1 collective-permute-start.5
  20.7 1.4 %shard_map.38.acc = f32[384,1536]{1,0:T(8,128)S(1)} custom-call(bf16[4,384,384]{2,1,0:T(8,128)(2,1)S(1)} %get-tuple-element.10.r, bf16[384,384]{1,0:T(8,128)(2,1)S(1)} %get-tuple-element.11.b), custom_call_target="tpu_custom_call" | custom-call | flops 905969664 | bytes 1179648 | tf_op jit(solution)/shard_map/pallas_call | solution.py:191
  22.1 1.4 %shard_map.39.acc = f32[384,1536]{1,0:T(8,128)S(1)} custom-call(f32[384,1536]{1,0:T(8,128)S(1)} %shard_map.38.acc, bf16[4,384,384]{2,1,0:T(8,128)(2,1)S(1)} %get-tuple-element.10.r, bf16[384,384]{1,0:T(8,128)(2,1)S(1)} %collective-permute-done.b), custom_call_target="tpu_custom_call", output_to_operand_aliasing={{}: (0, {})} | custom-call | flops 905969664 | bytes 1179648 | tf_op jit(solution)/shard_map/pallas_call | solution.py:212
  23.6 0.0 collective-permute-done.1.b
  23.6 1.4 %shard_map.40.acc = f32[384,1536]{1,0:T(8,128)S(1)} custom-call(f32[384,1536]{1,0:T(8,128)S(1)} %shard_map.39.acc, bf16[4,384,384]{2,1,0:T(8,128)(2,1)S(1)} %get-tuple-element.10.r, bf16[384,384]{1,0:T(8,128)(2,1)S(1)} %collective-permute-done.1.b), custom_call_target="tpu_custom_call", output_to_operand_aliasing={{}: (0, {})} | custom-call | flops 905969664 | bytes 1179648 | tf_op jit(solution)/shard_map/pallas_call | solution.py:212
  25.0 0.0 collective-permute-done.5.theirs
  25.0 2.6 %shard_map.44 = bf16[4,384,384]{2,1,0:T(8,128)(2,1)} custom-call(f32[384,1536]{1,0:T(8,128)S(1)} %shard_map.40.acc, bf16[4,384,384]{2,1,0:T(8,128)(2,1)S(1)} %get-tuple-element.10.r, bf16[256,384]{1,0:T(8,128)(2,1)S(1)} %shard_map.43.mine, bf16[256,384]{1,0:T(8,128)(2,1)S(1)} %collective-permute-done.5.theirs, bf16[4,384,128]{2,1,0:T(8,128)(2,1)S(1)} %get-tuple-element.14.u), custom_call_target="tpu_custom_call" | custom-call | flops 905969664 | bytes 1179648 | tf_op jit(solution)/shard_map/pallas_call | solution.py:215
  (2 shorter events, 0.1 us)
Async XLA Ops:
  0.0 13.2 %collective-permute-start = (bf16[384,384]{1,0:T(8,128)(2,1)}, bf16[384,384]{1,0:T(8,128)(2,1)S(1)}, u32[]{:S(2)}, u32[]{:S(2)}) collective-permute-start(bf16[384,384]{1,0:T(8,128)(2,1)} %bitcast.3), channel_id=1, source_target_pairs={{0,4},{1,13},{2,6},{3,15},{4,8},{5,1},{6,10},{7,3},{8,12},{9,5},{1... | collective-permute-start | bytes 884744 | tf_op jit(solution)/shard_map/ppermute | solution.py:171
  5.3 10.2 %collective-permute-start.2 = (f32[192,128]{1,0:T(8,128)S(1)}, f32[192,128]{1,0:T(8,128)S(1)}, u32[]{:S(2)}, u32[]{:S(2)}) collective-permute-start(f32[192,128]{1,0:T(8,128)S(1)} %get-tuple-element.13), channel_id=1, source_target_pairs={{0,1},{1,0},{2,3},{3,2},{4,5},{5,4},{6,7},{7,6},{8,9},{9,8},{10,11... | collective-permute-start | bytes 294920 | tf_op jit(solution)/shard_map/ppermute | solution.py:187
  7.8 7.6 %collective-permute-start.3 = (bf16[96,384]{1,0:T(8,128)(2,1)S(1)}, bf16[96,384]{1,0:T(8,128)(2,1)S(1)}, u32[]{:S(2)}, u32[]{:S(2)}) collective-permute-start(bf16[96,384]{1,0:T(8,128)(2,1)S(1)} %shard_map.41), channel_id=1, source_target_pairs={{0,8},{4,12},{8,0},{12,4},{1,9},{5,13},{9,1},{13,5},{2,10},{6,14},... | collective-permute-start | bytes 221192 | tf_op jit(solution)/shard_map/ppermute | solution.py:168
  13.2 10.3 %collective-permute-start.1 = (bf16[384,384]{1,0:T(8,128)(2,1)S(1)}, bf16[384,384]{1,0:T(8,128)(2,1)S(1)}, u32[]{:S(2)}, u32[]{:S(2)}) collective-permute-start(bf16[384,384]{1,0:T(8,128)(2,1)S(1)} %collective-permute-done.b), channel_id=1, source_target_pairs={{0,1},{1,0},{2,3},{3,2},{4,5},{5,4},{6,7},{7,6},{8,9},{9,8},{10,11... | collective-permute-start | bytes 884744 | tf_op jit(solution)/shard_map/ppermute | solution.py:208
  15.5 5.1 %collective-permute-start.4 = (bf16[160,384]{1,0:T(8,128)(2,1)S(1)}, bf16[160,384]{1,0:T(8,128)(2,1)S(1)}, u32[]{:S(2)}, u32[]{:S(2)}) collective-permute-start(bf16[160,384]{1,0:T(8,128)(2,1)S(1)} %shard_map.42.mine), channel_id=1, source_target_pairs={{0,2},{1,3},{2,0},{3,1},{4,6},{5,7},{6,4},{7,5},{8,10},{9,11},{10,... | collective-permute-start | bytes 368648 | tf_op jit(solution)/shard_map/ppermute | solution.py:195
  20.6 4.4 %collective-permute-start.5 = (bf16[256,384]{1,0:T(8,128)(2,1)S(1)}, bf16[256,384]{1,0:T(8,128)(2,1)S(1)}, u32[]{:S(2)}, u32[]{:S(2)}) collective-permute-start(bf16[256,384]{1,0:T(8,128)(2,1)S(1)} %shard_map.43.mine), channel_id=1, source_target_pairs={{0,1},{1,0},{2,3},{3,2},{4,5},{5,4},{6,7},{7,6},{8,9},{9,8},{10,11... | collective-permute-start | bytes 589832 | tf_op jit(solution)/shard_map/ppermute | solution.py:205

commit v3 on v2

v3 whole, which is shorter than its diff:
```python
import functools

import jax
import jax.numpy as jnp
from jax import lax
from jax.experimental import pallas as pl
from jax.experimental.pallas import tpu as pltpu
from jax.sharding import PartitionSpec as P

F32 = jnp.float32
BF16 = jnp.bfloat16
NT = (((1,), (1,)), ((), ()))
VMEM = pl.BlockSpec(memory_space=pltpu.VMEM)
HBM = pl.BlockSpec(memory_space=pltpu.HBM)


def call(kernel, outs, specs, scratch=(), aliases=None, flops=0, moved=0):
    return pl.pallas_call(
        kernel,
        out_shape=outs,
        in_specs=specs,
        out_specs=jax.tree.map(lambda o: VMEM if isinstance(o, pl.MemoryRef) else HBM, outs),
        scratch_shapes=scratch,
        input_output_aliases=aliases or {},
        cost_estimate=pl.CostEstimate(flops=flops, bytes_accessed=moved, transcendentals=0),
        compiler_params=pltpu.CompilerParams(vmem_limit_bytes=24 << 20),
    )


def in_hbm(x):
    return pltpu.with_memory_space_constraint(x, pltpu.HBM)


def mm(a, b):
    return jnp.dot(a, b, preferred_element_type=F32)


def mm_nt(a, b):
    return lax.dot_general(a, b, NT, preferred_element_type=F32)


def take_rows(where, src, *outs_and_sems):
    outs, sems = outs_and_sems[:2], outs_and_sems[2]
    copies = []
    for k, out in enumerate(outs):
        rows = out.shape[0]
        start = pl.multiple_of(where()[k] * rows, rows)
        copies.append(pltpu.make_async_copy(src.at[pl.ds(start, rows), :], out, sems.at[k]))
        copies[-1].start()
    for copy in copies:
        copy.wait()


def latent_part(first_j, r, u, out):
    j = first_j()
    acc = mm(r[0], u[j])
    for q in range(1, r.shape[0]):
        acc = acc + mm(r[q], u[j + q])
    out[...] = acc


def ladder_sum(r, factors, halfway):
    n, width, _ = r.shape
    rows = r[...].reshape(n * width, width)
    for p, b in enumerate(factors):
        h = mm_nt(b, rows).astype(BF16)
        for q in range(n):
            halfway[q * width : (q + 1) * width, p * width : (p + 1) * width] = h[:, q * width : (q + 1) * width]
    wide = factors[0] if len(factors) == 1 else jnp.concatenate(factors, 1)
    return mm_nt(wide, halfway[...])


def ladder_first(r, b, out, halfway):
    out[...] = ladder_sum(r, [b[...]], halfway)


def join(core, mine, theirs, whole):
    rows = mine.shape[0]
    whole[pl.ds(pl.multiple_of(core * rows, rows), rows), :] = mine[...]
    whole[pl.ds(pl.multiple_of((1 - core) * rows, rows), rows), :] = theirs[...]


def ladder_near(spot, acc, r, mine, theirs, out, whole, halfway):
    join(spot()[1], mine, theirs, whole)
    out[...] = acc[...] + ladder_sum(r, [whole[...]], halfway)


def pack(part, got, piece, out):
    rows, width = piece.shape
    rank = part.shape[1]
    out[:rows] = piece[...]
    total = (part[...] + got[...]).astype(BF16)
    deep = out.shape[0] - rows
    for k in range(width // rank):
        out[rows:, k * rank : (k + 1) * rank] = total[k * deep : (k + 1) * deep]


def repack(rows, mine, theirs, out):
    out[:rows] = mine[:rows]
    out[rows : 2 * rows] = theirs[:rows]
    out[2 * rows :] = (mine[rows:].astype(F32) + theirs[rows:].astype(F32)).astype(BF16)


def ladder_far(spot, first_j, rows, acc, r, mine, theirs, u, out, whole, latent, halfway):
    n, width, _ = r.shape
    parity, core = spot()
    for which, held in ((core, mine), (1 - core, theirs)):
        for k, half in enumerate((parity, 1 - parity)):
            at = pl.multiple_of((half * 2 + which) * rows, rows)
            whole[pl.ds(at, rows), :] = held[k * rows : (k + 1) * rows]
    folded = jnp.where(core == 0, mine[2 * rows :], theirs[2 * rows :])
    deep, rank = folded.shape[0], latent.shape[1]
    for k in range(width // rank):
        latent[k * deep : (k + 1) * deep] = folded[:, k * rank : (k + 1) * rank]
    out[...] = acc[...] + ladder_sum(r, [whole[...]], halfway)
    j = first_j()
    for q in range(n):
        cycle = mm_nt(latent[...], u[j + q]).astype(BF16)
        out[:, q * width : (q + 1) * width] += cycle.astype(F32)


def ladder_last(spot, acc, r, mine, theirs, out, whole, halfway, held, sems):
    n, width, _ = r.shape
    join(spot()[1], mine, theirs, whole)
    b = whole[...]
    h = mm_nt(b, r[...].reshape(n * width, width)).astype(BF16)
    for q in range(n):
        halfway[q * width : (q + 1) * width] = h[:, q * width : (q + 1) * width]
    copies = []
    for q in range(n):
        term = mm_nt(b, halfway[q * width : (q + 1) * width])
        held[q] = (acc[:, q * width : (q + 1) * width] + term).astype(BF16)
        copies.append(pltpu.make_async_copy(held.at[q], out.at[q], sems.at[q]))
        copies[-1].start()
    for copy in copies:
        copy.wait()


def sigma_block(n_i, n_j, doubles, aux_factors, cycle_factors):
    rows_i, cols_j, width, _ = doubles.shape
    pairs = rows_i * cols_j
    rank = cycle_factors.shape[-1]
    r = doubles.reshape(pairs, width, width)
    own = aux_factors.reshape(width, width)
    quarter, half = width // 4, width // 2
    fold = rank
    assert width % rank == 0 and fold * (width // rank) == width
    flops = 2 * pairs * width * width * width
    moved = 2 * pairs * width * width

    def spot():
        j = lax.axis_index("ja")
        return lax.rem(lax.div(j, 2) + lax.axis_index("grp"), 2), lax.rem(j, 2)

    def first_j():
        return lax.axis_index("ja") * cols_j

    def where():
        parity, core = spot()
        return parity * 2 + core, core

    def across(i, k):
        return i ^ k if n_i & (n_i - 1) == 0 else (i + k) % n_i

    core_swap = [(j, j ^ 1) for j in range(n_j)]
    chip_swap = [
        (g * n_j + j, (g ^ 1) * n_j + j if j % 2 else g * n_j + (j ^ 2)) for g in range(2) for j in range(n_j)
    ]
    far_away = n_i // 2

    piece, rows = call(
        functools.partial(take_rows, where),
        (pltpu.VMEM((quarter, width), BF16), pltpu.VMEM((half, width), BF16)),
        [HBM],
        [pltpu.SemaphoreType.DMA((2,))],
        flops=16 * flops,
        moved=8 * moved,
    )(in_hbm(own))
    piece = lax.ppermute(piece, "ia", [(i, across(i, far_away)) for i in range(n_i)])
    near = {}
    for k in range(1, n_i):
        if k != far_away:
            near[k] = lax.ppermute(rows, "ia", [(i, across(i, k)) for i in range(n_i)])

    part = call(
        functools.partial(latent_part, first_j),
        pltpu.VMEM((width, rank), F32),
        [VMEM] * 2,
        flops=flops * rank // width,
        moved=moved,
    )(r, cycle_factors)
    got = lax.ppermute(part, "ja", core_swap)

    wide = pltpu.VMEM((width, pairs * width), F32)
    whole = pltpu.VMEM((width, width), BF16)
    halfway = pltpu.VMEM((pairs * width, width), BF16)
    acc = call(ladder_first, wide, [VMEM] * 2, [halfway], flops=2 * flops, moved=moved)(r, own)

    packed = call(pack, pltpu.VMEM((quarter + fold, width), BF16), [VMEM] * 3)(part, got, piece)
    other = lax.ppermute(packed, ("grp", "ja"), chip_swap)
    packed = call(
        functools.partial(repack, quarter), pltpu.VMEM((2 * quarter + fold, width), BF16), [VMEM] * 2
    )(packed, other)
    apart = 4
    while apart < n_j:
        more = lax.ppermute(packed[2 * quarter :], "ja", [(j, j ^ apart) for j in range(n_j)])
        more = (packed[2 * quarter :].astype(F32) + more.astype(F32)).astype(BF16)
        packed = jnp.concatenate([packed[: 2 * quarter], more], 0)
        apart *= 2
    other = lax.ppermute(packed, "ja", core_swap)

    swapped = {}
    for k, mine in near.items():
        swapped[k] = lax.ppermute(mine, "ja", core_swap)
    *before, last = near
    for k in before:
        acc = call(
            functools.partial(ladder_near, spot),
            wide,
            [VMEM] * 4,
            [whole, halfway],
            {0: 0},
            flops=2 * flops,
            moved=moved,
        )(acc, r, near[k], swapped[k])
    acc = call(
        functools.partial(ladder_far, spot, first_j, quarter),
        wide,
        [VMEM] * 5,
        [whole, pltpu.VMEM((width, rank), BF16), halfway],
        {0: 0},
        flops=2 * flops,
        moved=moved,
    )(acc, r, packed, other, cycle_factors)
    out = call(
        functools.partial(ladder_last, spot),
        jax.ShapeDtypeStruct((pairs, width, width), BF16),
        [VMEM] * 4,
        [whole, halfway, pltpu.VMEM((pairs, width, width), BF16), pltpu.SemaphoreType.DMA((pairs,))],
        flops=2 * flops,
        moved=moved,
    )(acc, r, near[last], swapped[last])
    return out.reshape(doubles.shape)


def solution(mesh):
    n_i, n_j = mesh.shape["ia"], mesh.shape["ja"]
    in_specs = (P(("grp", "ia"), "ja", None, None), P("ia", None, None), P())
    out_specs = P(("grp", "ia"), "ja", None, None)

    def block(*args):
        return sigma_block(n_i, n_j, *args)

    return jax.shard_map(block, mesh=mesh, in_specs=in_specs, out_specs=out_specs, check_vma=False)
```

time: 27.8 us -> 32.6 us (1.17)
  starting transfers between devices: 7.55 us -> 10.4 us
  local copies, waits for them, and re-layouts: 0 us -> 2.69 us
  Pallas kernels: 10.1 us -> 8.6 us
  waiting for transfers between devices: 9.97 us -> 10.6 us
    ppermute x5 -> x7, starting transfers between devices: 7.48 us -> 10.3 us  [the longest x2 4.29 us: sigma_block(): near[k] = lax.ppermute(rows, 'ia', [(i, across(i, k)) for i in range(n_i)])]
    unnamed x0 -> x10, local copies, waits for them, and re-layouts: none -> 2.69 us
    pallas_call x6, Pallas kernels: 10 us -> 8.52 us  [the longest x1 2.33 us: sigma_block(): call(functools.partial(ladder_last, spot), jax.ShapeDtypeStruct((pairs, w...]
    ppermute x5 -> x7, waiting for transfers between devices: 9.97 us -> 10.6 us  [the longest x1 4.48 us: sigma_block(): lax.ppermute(piece, 'ia', [(i, across(i, far_away)) for i in range(n_i)])]
  transfers between devices with their start and end apart: 6 -> 8, of which waited for: 3 -> 3; matrix products, arithmetic and copies ran while one was open for 0% -> 0% of each run, Pallas kernels for 27% -> 18%
where the time goes in v3:
time: 32.6 us; the launch traced here: 32.3 us
  waiting for transfers between devices  10.6 us (33%)
  starting transfers between devices  10.4 us (32%)
  Pallas kernels  8.6 us (26%)
  local copies, waits for them, and re-layouts  2.69 us (8%)
    ppermute x1, waiting for transfers between devices, sigma_block(): lax.ppermute(piece, 'ia', [(i, across(i, far_away)) for i in range(n_i)])  4.48 us
    ppermute x2, starting transfers between devices, sigma_block(): near[k] = lax.ppermute(rows, 'ia', [(i, across(i, k)) for i in range(n_i)])  4.29 us
    ppermute x1, starting transfers between devices, sigma_block(): lax.ppermute(piece, 'ia', [(i, across(i, far_away)) for i in range(n_i)])  3.68 us
    ppermute x1, waiting for transfers between devices, sigma_block(): other = lax.ppermute(packed, ('grp', 'ja'), chip_swap)  3.18 us
    ppermute x2, waiting for transfers between devices, sigma_block(): near[k] = lax.ppermute(rows, 'ia', [(i, across(i, k)) for i in range(n_i)])  2.94 us
    unnamed x10, local copies, waits for them, and re-layouts  2.69 us
    pallas_call x1, Pallas kernels, sigma_block(): call(functools.partial(ladder_last, spot), jax.ShapeDtypeStruct((pairs, w...  2.33 us
    pallas_call x1, Pallas kernels, sigma_block(): call(functools.partial(ladder_far, spot, first_j, quarter), wide, [VMEM]...  1.79 us
  transfers between devices with their start and end apart: 8, of which 3 were waited for; matrix products, arithmetic and copies ran while one was open for 0% of the time, Pallas kernels for 18%

profile of v3, /device:TPU:0, one launch (start us, length us, event | category | flops | bytes accessed | tf_op | source)
XLA Modules:
  0.0 32.3 jit_solution(6014011180855386682)
XLA Ops:
  0.0 0.0 copy-start
  0.0 1.3 %copy-done = bf16[1,4,384,384]{3,2,1,0:T(8,128)(2,1)S(1)} copy-done((bf16[1,4,384,384]{3,2,1,0:T(8,128)(2,1)S(1)}, bf16[1,4,384,384]{3,2,1,0:T(8,128)(2,1)}, u32[]{:S(2)}) %copy-start) | copy-done | bytes 1179672
  1.3 0.0 copy-start.2
  1.3 1.4 %copy-done.2 = bf16[16,384,128]{2,1,0:T(8,128)(2,1)S(1)} copy-done((bf16[16,384,128]{2,1,0:T(8,128)(2,1)S(1)}, bf16[16,384,128]{2,1,0:T(8,128)(2,1)}, u32[]{:S(2)}) %copy-start.2) | copy-done | bytes 1572888
  2.7 0.5 %shard_map.40.part = f32[384,128]{1,0:T(8,128)S(1)} custom-call(bf16[4,384,384]{2,1,0:T(8,128)(2,1)S(1)} %bitcast.3, bf16[16,384,128]{2,1,0:T(8,128)(2,1)S(1)} %copy-done.2), custom_call_target="tpu_custom_call" | custom-call | flops 150994944 | bytes 1179648 | tf_op jit(solution)/shard_map/pallas_call | solution.py:185
  3.2 0.6 %collective-permute-start.2 = (f32[384,128]{1,0:T(8,128)S(1)}, f32[384,128]{1,0:T(8,128)S(1)}, u32[]{:S(2)}, u32[]{:S(2)}) collective-permute-start(f32[384,128]{1,0:T(8,128)S(1)} %shard_map.40.part), channel_id=1, source_target_pairs={{0,1},{1,0},{2,3},{3,2},{4,5},{5,4},{6,7},{7,6},{8,9},{9,8},{10,11... | collective-permute-start | bytes 589832 | tf_op jit(solution)/shard_map/ppermute | solution.py:192
  3.7 0.0 copy-start.1
  3.7 0.0 copy-start.4
  3.7 1.1 %shard_map.38 = (bf16[96,384]{1,0:T(8,128)(2,1)S(1)}, bf16[192,384]{1,0:T(8,128)(2,1)S(1)}) custom-call(bf16[384,384]{1,0:T(8,128)(2,1)} %bitcast.8), custom_call_target="tpu_custom_call" | custom-call | flops 7247757312 | bytes 9437184 | tf_op jit(solution)/shard_map/pallas_call | solution.py:171
  4.8 3.7 %collective-permute-start.3 = (bf16[96,384]{1,0:T(8,128)(2,1)S(1)}, bf16[96,384]{1,0:T(8,128)(2,1)S(1)}, u32[]{:S(2)}, u32[]{:S(2)}) collective-permute-start(bf16[96,384]{1,0:T(8,128)(2,1)S(1)} %get-tuple-element.8), channel_id=1, source_target_pairs={{0,8},{4,12},{8,0},{12,4},{1,9},{5,13},{9,1},{13,5},{2,10},{6,14},... | collective-permute-start | bytes 221192 | tf_op jit(solution)/shard_map/ppermute | solution.py:179
  8.5 4.5 %collective-permute-done.3.piece = bf16[96,384]{1,0:T(8,128)(2,1)S(1)} collective-permute-done((bf16[96,384]{1,0:T(8,128)(2,1)S(1)}, bf16[96,384]{1,0:T(8,128)(2,1)S(1)}, u32[]{:S(2)}, u32[]{:S(2)}) %collective-permute-start.3) | collective-permute-done | bytes 73760 | tf_op jit(solution)/shard_map/ppermute | solution.py:179
  13.0 0.0 collective-permute-done.2.got
  13.0 1.6 %collective-permute-start.4 = (bf16[224,384]{1,0:T(8,128)(2,1)S(1)}, bf16[224,384]{1,0:T(8,128)(2,1)S(1)}, u32[]{:S(2)}, u32[]{:S(2)}) collective-permute-start(bf16[224,384]{1,0:T(8,128)(2,1)S(1)} %shard_map.41.mine), channel_id=1, source_target_pairs={{0,2},{1,17},{2,0},{3,19},{16,18},{17,1},{18,16},{19,3},{4,6},{5,2... | collective-permute-start | bytes 516104 | tf_op jit(solution)/shard_map/ppermute | solution.py:200
  14.6 0.7 %collective-permute-start = (bf16[192,384]{1,0:T(8,128)(2,1)S(1)}, bf16[192,384]{1,0:T(8,128)(2,1)S(1)}, u32[]{:S(2)}, u32[]{:S(2)}) collective-permute-start(bf16[192,384]{1,0:T(8,128)(2,1)S(1)} %get-tuple-element.7), channel_id=1, source_target_pairs={{0,4},{4,0},{8,12},{12,8},{1,5},{5,1},{9,13},{13,9},{2,6},{6,2},{1... | collective-permute-start | bytes 442376 | tf_op jit(solution)/shard_map/ppermute | solution.py:183
  15.3 3.2 %collective-permute-done.4.theirs = bf16[224,384]{1,0:T(8,128)(2,1)S(1)} collective-permute-done((bf16[224,384]{1,0:T(8,128)(2,1)S(1)}, bf16[224,384]{1,0:T(8,128)(2,1)S(1)}, u32[]{:S(2)}, u32[]{:S(2)}) %collective-permute-start.4) | collective-permute-done | bytes 172064 | tf_op jit(solution)/shard_map/ppermute | solution.py:200
  18.5 0.1 collective-permute-start.5
  18.6 3.6 %collective-permute-start.6 = (bf16[192,384]{1,0:T(8,128)(2,1)S(1)}, bf16[192,384]{1,0:T(8,128)(2,1)S(1)}, u32[]{:S(2)}, u32[]{:S(2)}) collective-permute-start(bf16[192,384]{1,0:T(8,128)(2,1)S(1)} %get-tuple-element.7), channel_id=1, source_target_pairs={{0,12},{4,8},{8,4},{12,0},{1,13},{5,9},{9,5},{13,1},{2,14},{6,10},... | collective-permute-start | bytes 442376 | tf_op jit(solution)/shard_map/ppermute | solution.py:183
  22.2 0.0 collective-permute-done.mine
  22.2 0.2 collective-permute-start.1
  22.4 0.0 copy-done.1
  22.4 0.0 copy-done.4
  22.4 1.4 %shard_map.37.acc = f32[384,1536]{1,0:T(8,128)S(1)} custom-call(bf16[4,384,384]{2,1,0:T(8,128)(2,1)S(1)} %bitcast.4, bf16[384,384]{1,0:T(8,128)(2,1)S(1)} %bitcast.9), custom_call_target="tpu_custom_call" | custom-call | flops 905969664 | bytes 1179648 | tf_op jit(solution)/shard_map/pallas_call | solution.py:197
  23.8 0.0 copy-start.3
  23.8 2.9 %collective-permute-done.6.mine = bf16[192,384]{1,0:T(8,128)(2,1)S(1)} collective-permute-done((bf16[192,384]{1,0:T(8,128)(2,1)S(1)}, bf16[192,384]{1,0:T(8,128)(2,1)S(1)}, u32[]{:S(2)}, u32[]{:S(2)}) %collective-permute-start.6) | collective-permute-done | bytes 147488 | tf_op jit(solution)/shard_map/ppermute | solution.py:183
  26.7 0.0 collective-permute-start.7
  26.7 0.0 collective-permute-done.1.theirs
  26.7 1.4 %shard_map.39.acc = f32[384,1536]{1,0:T(8,128)S(1)} custom-call(f32[384,1536]{1,0:T(8,128)S(1)} %shard_map.37.acc, bf16[4,384,384]{2,1,0:T(8,128)(2,1)S(1)} %bitcast.5, bf16[192,384]{1,0:T(8,128)(2,1)S(1)} %collective-permute-done.mine, bf16[192,384]{1,0:T(8,128)(2,1)S(1)} %collective-permute-done.1.theirs), custom_call_target="tpu_custom_call", output_to_operand_aliasing={{}: (0, {})} | custom-call | flops 905969664 | bytes 1179648 | tf_op jit(solution)/shard_map/pallas_call | solution.py:217
  28.2 0.0 collective-permute-done.5.theirs
  28.2 0.0 copy-done.3
  28.2 1.8 %shard_map.43.acc = f32[384,1536]{1,0:T(8,128)S(1)} custom-call(f32[384,1536]{1,0:T(8,128)S(1)} %shard_map.39.acc, bf16[4,384,384]{2,1,0:T(8,128)(2,1)S(1)} %bitcast.6, bf16[320,384]{1,0:T(8,128)(2,1)S(1)} %shard_map.42.mine, bf16[320,384]{1,0:T(8,128)(2,1)S(1)} %collective-permute-done.5.theirs, ...), custom_call_target="tpu_custom_call", output_to_operand_aliasing={{}: (0, {})} | custom-call | flops 905969664 | bytes 1179648 | tf_op jit(solution)/shard_map/pallas_call | solution.py:226
  30.0 0.0 collective-permute-done.7.theirs
  30.0 2.3 %shard_map.44 = bf16[4,384,384]{2,1,0:T(8,128)(2,1)} custom-call(f32[384,1536]{1,0:T(8,128)S(1)} %shard_map.43.acc, bf16[4,384,384]{2,1,0:T(8,128)(2,1)S(1)} %bitcast.7, bf16[192,384]{1,0:T(8,128)(2,1)S(1)} %collective-permute-done.6.mine, bf16[192,384]{1,0:T(8,128)(2,1)S(1)} %collective-permute-done.7.theirs), custom_call_target="tpu_custom_call" | custom-call | flops 905969664 | bytes 1179648 | tf_op jit(solution)/shard_map/pallas_call | solution.py:235
  (2 shorter events, 0.1 us)
Async XLA Ops:
  0.0 1.3 %copy-start = (bf16[1,4,384,384]{3,2,1,0:T(8,128)(2,1)S(1)}, bf16[1,4,384,384]{3,2,1,0:T(8,128)(2,1)}, u32[]{:S(2)}) copy-start(bf16[1,4,384,384]{3,2,1,0:T(8,128)(2,1)} %param.3) | copy-start | bytes 3538948
  1.3 1.4 %copy-start.2 = (bf16[16,384,128]{2,1,0:T(8,128)(2,1)S(1)}, bf16[16,384,128]{2,1,0:T(8,128)(2,1)}, u32[]{:S(2)}) copy-start(bf16[16,384,128]{2,1,0:T(8,128)(2,1)} %u.3) | copy-start | bytes 4718596
  3.2 9.8 %collective-permute-start.2 = (f32[384,128]{1,0:T(8,128)S(1)}, f32[384,128]{1,0:T(8,128)S(1)}, u32[]{:S(2)}, u32[]{:S(2)}) collective-permute-start(f32[384,128]{1,0:T(8,128)S(1)} %shard_map.40.part), channel_id=1, source_target_pairs={{0,1},{1,0},{2,3},{3,2},{4,5},{5,4},{6,7},{7,6},{8,9},{9,8},{10,11... | collective-permute-start | bytes 589832 | tf_op jit(solution)/shard_map/ppermute | solution.py:192
  3.7 18.6 %copy-start.1 = (bf16[1,4,384,384]{3,2,1,0:T(8,128)(2,1)S(1)}, bf16[1,4,384,384]{3,2,1,0:T(8,128)(2,1)}, u32[]{:S(2)}) copy-start(bf16[1,4,384,384]{3,2,1,0:T(8,128)(2,1)} %param.3) | copy-start | bytes 3538948
  3.7 18.6 %copy-start.4 = (bf16[1,384,384]{2,1,0:T(8,128)(2,1)S(1)}, bf16[1,384,384]{2,1,0:T(8,128)(2,1)}, u32[]{:S(2)}) copy-start(bf16[1,384,384]{2,1,0:T(8,128)(2,1)} %param.4) | copy-start | bytes 884740
  4.8 8.2 %collective-permute-start.3 = (bf16[96,384]{1,0:T(8,128)(2,1)S(1)}, bf16[96,384]{1,0:T(8,128)(2,1)S(1)}, u32[]{:S(2)}, u32[]{:S(2)}) collective-permute-start(bf16[96,384]{1,0:T(8,128)(2,1)S(1)} %get-tuple-element.8), channel_id=1, source_target_pairs={{0,8},{4,12},{8,0},{12,4},{1,9},{5,13},{9,1},{13,5},{2,10},{6,14},... | collective-permute-start | bytes 221192 | tf_op jit(solution)/shard_map/ppermute | solution.py:179
  13.0 5.5 %collective-permute-start.4 = (bf16[224,384]{1,0:T(8,128)(2,1)S(1)}, bf16[224,384]{1,0:T(8,128)(2,1)S(1)}, u32[]{:S(2)}, u32[]{:S(2)}) collective-permute-start(bf16[224,384]{1,0:T(8,128)(2,1)S(1)} %shard_map.41.mine), channel_id=1, source_target_pairs={{0,2},{1,17},{2,0},{3,19},{16,18},{17,1},{18,16},{19,3},{4,6},{5,2... | collective-permute-start | bytes 516104 | tf_op jit(solution)/shard_map/ppermute | solution.py:200
  14.6 7.6 %collective-permute-start = (bf16[192,384]{1,0:T(8,128)(2,1)S(1)}, bf16[192,384]{1,0:T(8,128)(2,1)S(1)}, u32[]{:S(2)}, u32[]{:S(2)}) collective-permute-start(bf16[192,384]{1,0:T(8,128)(2,1)S(1)} %get-tuple-element.7), channel_id=1, source_target_pairs={{0,4},{4,0},{8,12},{12,8},{1,5},{5,1},{9,13},{13,9},{2,6},{6,2},{1... | collective-permute-start | bytes 442376 | tf_op jit(solution)/shard_map/ppermute | solution.py:183
  18.5 9.7 %collective-permute-start.5 = (bf16[320,384]{1,0:T(8,128)(2,1)S(1)}, bf16[320,384]{1,0:T(8,128)(2,1)S(1)}, u32[]{:S(2)}, u32[]{:S(2)}) collective-permute-start(bf16[320,384]{1,0:T(8,128)(2,1)S(1)} %shard_map.42.mine), channel_id=1, source_target_pairs={{0,1},{1,0},{2,3},{3,2},{4,5},{5,4},{6,7},{7,6},{8,9},{9,8},{10,11... | collective-permute-start | bytes 737288 | tf_op jit(solution)/shard_map/ppermute | solution.py:210
  18.6 8.1 %collective-permute-start.6 = (bf16[192,384]{1,0:T(8,128)(2,1)S(1)}, bf16[192,384]{1,0:T(8,128)(2,1)S(1)}, u32[]{:S(2)}, u32[]{:S(2)}) collective-permute-start(bf16[192,384]{1,0:T(8,128)(2,1)S(1)} %get-tuple-element.7), channel_id=1, source_target_pairs={{0,12},{4,8},{8,4},{12,0},{1,13},{5,9},{9,5},{13,1},{2,14},{6,10},... | collective-permute-start | bytes 442376 | tf_op jit(solution)/shard_map/ppermute | solution.py:183
  22.2 4.5 %collective-permute-start.1 = (bf16[192,384]{1,0:T(8,128)(2,1)S(1)}, bf16[192,384]{1,0:T(8,128)(2,1)S(1)}, u32[]{:S(2)}, u32[]{:S(2)}) collective-permute-start(bf16[192,384]{1,0:T(8,128)(2,1)S(1)} %collective-permute-done.mine), channel_id=1, source_target_pairs={{0,1},{1,0},{2,3},{3,2},{4,5},{5,4},{6,7},{7,6},{8,9},{9,8},{10,11... | collective-permute-start | bytes 442376 | tf_op jit(solution)/shard_map/ppermute | solution.py:214
  23.8 4.4 %copy-start.3 = (bf16[16,384,128]{2,1,0:T(8,128)(2,1)S(1)}, bf16[16,384,128]{2,1,0:T(8,128)(2,1)}, u32[]{:S(2)}) copy-start(bf16[16,384,128]{2,1,0:T(8,128)(2,1)} %u.3) | copy-start | bytes 4718596
  26.7 3.3 %collective-permute-start.7 = (bf16[192,384]{1,0:T(8,128)(2,1)S(1)}, bf16[192,384]{1,0:T(8,128)(2,1)S(1)}, u32[]{:S(2)}, u32[]{:S(2)}) collective-permute-start(bf16[192,384]{1,0:T(8,128)(2,1)S(1)} %collective-permute-done.6.mine), channel_id=1, source_target_pairs={{0,1},{1,0},{2,3},{3,2},{4,5},{5,4},{6,7},{7,6},{8,9},{9,8},{10,11... | collective-permute-start | bytes 442376 | tf_op jit(solution)/shard_map/ppermute | solution.py:214

commit v4 on v3

--- a/solution.py
+++ b/solution.py
@@ -39,16 +39,26 @@
     return lax.dot_general(a, b, NT, preferred_element_type=F32)
 
 
-def take_rows(where, src, *outs_and_sems):
-    outs, sems = outs_and_sems[:2], outs_and_sems[2]
-    copies = []
-    for k, out in enumerate(outs):
-        rows = out.shape[0]
-        start = pl.multiple_of(where()[k] * rows, rows)
-        copies.append(pltpu.make_async_copy(src.at[pl.ds(start, rows), :], out, sems.at[k]))
-        copies[-1].start()
+def take_far(index_of, src, out, sems):
+    rows = out.shape[0] // 3
+    start = index_of() * out.shape[0]
+    copies = [
+        pltpu.make_async_copy(
+            src.at[pl.ds(pl.multiple_of(start + k * rows, rows), rows), :],
+            out.at[pl.ds(k * rows, rows), :],
+            sems.at[k],
+        )
+        for k in range(3)
+    ]
+    for copy in copies:
+        copy.start()
     for copy in copies:
         copy.wait()
+
+
+def take_near(index_of, src, out):
+    rows = out.shape[0]
+    out[...] = src[pl.ds(pl.multiple_of(index_of() * rows, rows), rows), :]
 
 
 def latent_part(first_j, r, u, out):
@@ -101,37 +111,59 @@
     out[2 * rows :] = (mine[rows:].astype(F32) + theirs[rows:].astype(F32)).astype(BF16)
 
 
-def ladder_far(spot, first_j, rows, acc, r, mine, theirs, u, out, whole, latent, halfway):
+def first_products(r, pieces, halfway):
     n, width, _ = r.shape
-    parity, core = spot()
-    for which, held in ((core, mine), (1 - core, theirs)):
-        for k, half in enumerate((parity, 1 - parity)):
-            at = pl.multiple_of((half * 2 + which) * rows, rows)
-            whole[pl.ds(at, rows), :] = held[k * rows : (k + 1) * rows]
-    folded = jnp.where(core == 0, mine[2 * rows :], theirs[2 * rows :])
+    stack = jnp.concatenate([rows for rows, _, _ in pieces], 0)
+    for g in range(0, n, 2):
+        h = mm_nt(stack, r[g : g + 2].reshape(2 * width, width)).astype(BF16)
+        top = 0
+        for rows, p, start in pieces:
+            size = rows.shape[0]
+            for k in range(2):
+                at = pl.multiple_of((g + k) * width + start, size)
+                halfway[pl.ds(at, size), p * width : (p + 1) * width] = h[top : top + size, k * width : (k + 1) * width]
+            top += size
+
+
+def held_rows(spot, rows, which, packed, near):
+    parity, _ = spot()
+    half = near.shape[0]
+    return [
+        (packed[:rows], 0, (parity * 2 + which) * rows),
+        (packed[rows : 2 * rows], 0, ((1 - parity) * 2 + which) * rows),
+        (near[...], 1, which * half),
+    ]
+
+
+def ladder_ahead(spot, rows, r, packed, near, halfway):
+    first_products(r, held_rows(spot, rows, spot()[1], packed, near), halfway)
+
+
+def ladder_last(
+    spot, first_j, rows, acc, r, packed, other, near, swapped, u, ahead, out, halfway, wide, latent, held, sems
+):
+    n, width, _ = r.shape
+    core = spot()[1]
+    theirs = held_rows(spot, rows, 1 - core, other, swapped)
+    first_products(r, theirs, halfway)
+    for piece, p, start in held_rows(spot, rows, core, packed, near) + theirs:
+        size = piece.shape[0]
+        wide[pl.ds(pl.multiple_of(start, size), size), p * width : (p + 1) * width] = piece
+    folded = jnp.where(core == 0, packed[2 * rows :], other[2 * rows :])
     deep, rank = folded.shape[0], latent.shape[1]
     for k in range(width // rank):
         latent[k * deep : (k + 1) * deep] = folded[:, k * rank : (k + 1) * rank]
-    out[...] = acc[...] + ladder_sum(r, [whole[...]], halfway)
     j = first_j()
-    for q in range(n):
-        cycle = mm_nt(latent[...], u[j + q]).astype(BF16)
-        out[:, q * width : (q + 1) * width] += cycle.astype(F32)
-
-
-def ladder_last(spot, acc, r, mine, theirs, out, whole, halfway, held, sems):
-    n, width, _ = r.shape
-    join(spot()[1], mine, theirs, whole)
-    b = whole[...]
-    h = mm_nt(b, r[...].reshape(n * width, width)).astype(BF16)
-    for q in range(n):
-        halfway[q * width : (q + 1) * width] = h[:, q * width : (q + 1) * width]
     copies = []
-    for q in range(n):
-        term = mm_nt(b, halfway[q * width : (q + 1) * width])
-        held[q] = (acc[:, q * width : (q + 1) * width] + term).astype(BF16)
-        copies.append(pltpu.make_async_copy(held.at[q], out.at[q], sems.at[q]))
-        copies[-1].start()
+    for g in range(0, n, 2):
+        span = slice(g * width, (g + 2) * width)
+        term = mm_nt(wide[...], halfway[span])
+        cycle = mm_nt(latent[...], u[pl.ds(j + g, 2)].reshape(2 * width, rank)).astype(BF16)
+        total = (acc[:, span] + term + cycle.astype(F32)).astype(BF16)
+        for k in range(2):
+            held[g + k] = total[:, k * width : (k + 1) * width]
+            copies.append(pltpu.make_async_copy(held.at[g + k], out.at[g + k], sems.at[g + k]))
+            copies[-1].start()
     for copy in copies:
         copy.wait()
 
@@ -155,9 +187,9 @@
     def first_j():
         return lax.axis_index("ja") * cols_j
 
-    def where():
+    def quarter_of():
         parity, core = spot()
-        return parity * 2 + core, core
+        return parity * 2 + core
 
     def across(i, k):
         return i ^ k if n_i & (n_i - 1) == 0 else (i + k) % n_i
@@ -168,15 +200,22 @@
     ]
     far_away = n_i // 2
 
-    piece, rows = call(
-        functools.partial(take_rows, where),
-        (pltpu.VMEM((quarter, width), BF16), pltpu.VMEM((half, width), BF16)),
+    piece = call(
+        functools.partial(take_far, quarter_of),
+        pltpu.VMEM((quarter, width), BF16),
         [HBM],
-        [pltpu.SemaphoreType.DMA((2,))],
+        [pltpu.SemaphoreType.DMA((3,))],
+        flops=2 * flops,
+        moved=moved * 2 // 2,
+    )(in_hbm(own))
+    piece = lax.ppermute(piece, "ia", [(i, across(i, far_away)) for i in range(n_i)])
+    rows = call(
+        functools.partial(take_near, lambda: spot()[1]),
+        pltpu.VMEM((half, width), BF16),
+        [VMEM],
         flops=16 * flops,
         moved=8 * moved,
-    )(in_hbm(own))
-    piece = lax.ppermute(piece, "ia", [(i, across(i, far_away)) for i in range(n_i)])
+    )(own)
     near = {}
     for k in range(1, n_i):
         if k != far_away:
@@ -223,23 +262,27 @@
             flops=2 * flops,
             moved=moved,
         )(acc, r, near[k], swapped[k])
-    acc = call(
-        functools.partial(ladder_far, spot, first_j, quarter),
-        wide,
-        [VMEM] * 5,
-        [whole, pltpu.VMEM((width, rank), BF16), halfway],
-        {0: 0},
-        flops=2 * flops,
+    ahead = call(
+        functools.partial(ladder_ahead, spot, quarter),
+        pltpu.VMEM((pairs * width, 2 * width), BF16),
+        [VMEM] * 3,
+        flops=flops,
         moved=moved,
-    )(acc, r, packed, other, cycle_factors)
-    out = call(
-        functools.partial(ladder_last, spot),
-        jax.ShapeDtypeStruct((pairs, width, width), BF16),
-        [VMEM] * 4,
-        [whole, halfway, pltpu.VMEM((pairs, width, width), BF16), pltpu.SemaphoreType.DMA((pairs,))],
-        flops=2 * flops,
-        moved=moved,
-    )(acc, r, near[last], swapped[last])
+    )(r, packed, near[last])
+    out, _ = call(
+        functools.partial(ladder_last, spot, first_j, quarter),
+        (jax.ShapeDtypeStruct((pairs, width, width), BF16), pltpu.VMEM((pairs * width, 2 * width), BF16)),
+        [VMEM] * 8,
+        [
+            pltpu.VMEM((width, 2 * width), BF16),
+            pltpu.VMEM((width, rank), BF16),
+            pltpu.VMEM((pairs, width, width), BF16),
+            pltpu.SemaphoreType.DMA((pairs,)),
+        ],
+        {7: 1},
+        flops=3 * flops,
+        moved=2 * moved,
+    )(acc, r, packed, other, near[last], swapped[last], cycle_factors, ahead)
     return out.reshape(doubles.shape)
 
 

time: 32.6 us -> 24.6 us (0.75)
  waiting for transfers between devices: 10.6 us -> 5.04 us
  local copies, waits for them, and re-layouts: 2.69 us -> 0.01 us
  starting transfers between devices: 10.4 us -> 11.2 us
  Pallas kernels: 8.6 us -> 8.04 us
    ppermute x1, waiting for transfers between devices: 3.18 us -> 0.35 us  [sigma_block(): other = lax.ppermute(packed, ('grp', 'ja'), chip_swap)]
    ppermute x1, waiting for transfers between devices: 4.48 us -> 1.69 us  [sigma_block(): lax.ppermute(piece, 'ia', [(i, across(i, far_away)) for i in range(n_i)])]
    unnamed x10 -> x6, local copies, waits for them, and re-layouts: 2.69 us -> 0.01 us
    ppermute x2, starting transfers between devices: 4.29 us -> 4.97 us  [sigma_block(): near[k] = lax.ppermute(rows, 'ia', [(i, across(i, k)) for i in range(n_i)])]
    pallas_call x3 -> x4, Pallas kernels: 5.19 us -> 4.66 us  [the longest x1 2.88 us: sigma_block(): call(functools.partial(ladder_last, spot, first_j, quarter), (jax.ShapeDt...]
    ppermute x1, starting transfers between devices: 0.56 us -> 0.07 us  [sigma_block(): got = lax.ppermute(part, 'ja', core_swap)]
    ppermute x1, starting transfers between devices: 3.68 us -> 4.15 us  [sigma_block(): lax.ppermute(piece, 'ia', [(i, across(i, far_away)) for i in range(n_i)])]
  transfers between devices with their start and end apart: 8 -> 8, of which waited for: 3 -> 3; matrix products, arithmetic and copies ran while one was open for 0% -> 0% of each run, Pallas kernels for 18% -> 17%
where the time goes in v4:
time: 24.6 us; the launch traced here: 24.4 us
  starting transfers between devices  11.2 us (46%)
  Pallas kernels  8.04 us (33%)
  waiting for transfers between devices  5.04 us (20%)
    ppermute x2, starting transfers between devices, sigma_block(): near[k] = lax.ppermute(rows, 'ia', [(i, across(i, k)) for i in range(n_i)])  4.97 us
    ppermute x1, starting transfers between devices, sigma_block(): lax.ppermute(piece, 'ia', [(i, across(i, far_away)) for i in range(n_i)])  4.15 us
    ppermute x2, waiting for transfers between devices, sigma_block(): near[k] = lax.ppermute(rows, 'ia', [(i, across(i, k)) for i in range(n_i)])  2.99 us
    pallas_call x1, Pallas kernels, sigma_block(): call(functools.partial(ladder_last, spot, first_j, quarter), (jax.ShapeDt...  2.88 us
    ppermute x1, starting transfers between devices, sigma_block(): other = lax.ppermute(packed, ('grp', 'ja'), chip_swap)  1.79 us
    ppermute x1, waiting for transfers between devices, sigma_block(): lax.ppermute(piece, 'ia', [(i, across(i, far_away)) for i in range(n_i)])  1.69 us
    pallas_call x1, Pallas kernels, sigma_block(): call(functools.partial(ladder_near, spot), wide, [VMEM] * 4, [whole, half...  1.43 us
    pallas_call x1, Pallas kernels, sigma_block(): call(ladder_first, wide, [VMEM] * 2, [halfway], flops=2 * flops, moved=mo...  1.41 us
  transfers between devices with their start and end apart: 8, of which 3 were waited for; matrix products, arithmetic and copies ran while one was open for 0% of the time, Pallas kernels for 17%

profile of v4, /device:TPU:0, one launch (start us, length us, event | category | flops | bytes accessed | tf_op | source)
XLA Modules:
  0.0 24.4 jit_solution(4627184525295371088)
XLA Ops:
  0.0 0.0 copy-start.1
  0.0 0.0 copy-start
  0.0 0.0 copy-start.2
  0.0 0.9 %shard_map.41 = bf16[96,384]{1,0:T(8,128)(2,1)S(1)} custom-call(bf16[384,384]{1,0:T(8,128)(2,1)} %bitcast.8), custom_call_target="tpu_custom_call" | custom-call | flops 905969664 | bytes 1179648 | tf_op jit(solution)/shard_map/pallas_call | solution.py:203
  1.0 4.2 %collective-permute-start.3 = (bf16[96,384]{1,0:T(8,128)(2,1)S(1)}, bf16[96,384]{1,0:T(8,128)(2,1)S(1)}, u32[]{:S(2)}, u32[]{:S(2)}) collective-permute-start(bf16[96,384]{1,0:T(8,128)(2,1)S(1)} %shard_map.41), channel_id=1, source_target_pairs={{0,8},{4,12},{8,0},{12,4},{1,9},{5,13},{9,1},{13,5},{2,10},{6,14},... | collective-permute-start | bytes 221192 | tf_op jit(solution)/shard_map/ppermute | solution.py:211
  5.1 0.0 copy-done.1
  5.1 0.0 copy-done
  5.1 0.5 %shard_map.40.part = f32[384,128]{1,0:T(8,128)S(1)} custom-call(bf16[4,384,384]{2,1,0:T(8,128)(2,1)S(1)} %bitcast.3, bf16[16,384,128]{2,1,0:T(8,128)(2,1)S(1)} %copy-done.1), custom_call_target="tpu_custom_call" | custom-call | flops 150994944 | bytes 1179648 | tf_op jit(solution)/shard_map/pallas_call | solution.py:224
  5.6 0.1 collective-permute-start.2
  5.7 0.0 copy-done.2
  5.7 1.6 %collective-permute-start = (bf16[192,384]{1,0:T(8,128)(2,1)S(1)}, bf16[192,384]{1,0:T(8,128)(2,1)S(1)}, u32[]{:S(2)}, u32[]{:S(2)}) collective-permute-start(bf16[192,384]{1,0:T(8,128)(2,1)S(1)} %shard_map.38), channel_id=1, source_target_pairs={{0,4},{4,0},{8,12},{12,8},{1,5},{5,1},{9,13},{13,9},{2,6},{6,2},{1... | collective-permute-start | bytes 442376 | tf_op jit(solution)/shard_map/ppermute | solution.py:222
  7.4 1.7 %collective-permute-done.3.piece = bf16[96,384]{1,0:T(8,128)(2,1)S(1)} collective-permute-done((bf16[96,384]{1,0:T(8,128)(2,1)S(1)}, bf16[96,384]{1,0:T(8,128)(2,1)S(1)}, u32[]{:S(2)}, u32[]{:S(2)}) %collective-permute-start.3) | collective-permute-done | bytes 73760 | tf_op jit(solution)/shard_map/ppermute | solution.py:211
  9.0 0.0 collective-permute-done.2.got
  9.1 1.8 %collective-permute-start.4 = (bf16[224,384]{1,0:T(8,128)(2,1)S(1)}, bf16[224,384]{1,0:T(8,128)(2,1)S(1)}, u32[]{:S(2)}, u32[]{:S(2)}) collective-permute-start(bf16[224,384]{1,0:T(8,128)(2,1)S(1)} %shard_map.42.mine), channel_id=1, source_target_pairs={{0,2},{1,17},{2,0},{3,19},{16,18},{17,1},{18,16},{19,3},{4,6},{5,2... | collective-permute-start | bytes 516104 | tf_op jit(solution)/shard_map/ppermute | solution.py:239
  10.9 3.3 %collective-permute-start.6 = (bf16[192,384]{1,0:T(8,128)(2,1)S(1)}, bf16[192,384]{1,0:T(8,128)(2,1)S(1)}, u32[]{:S(2)}, u32[]{:S(2)}) collective-permute-start(bf16[192,384]{1,0:T(8,128)(2,1)S(1)} %shard_map.38), channel_id=1, source_target_pairs={{0,12},{4,8},{8,4},{12,0},{1,13},{5,9},{9,5},{13,1},{2,14},{6,10},... | collective-permute-start | bytes 442376 | tf_op jit(solution)/shard_map/ppermute | solution.py:222
  14.2 0.0 collective-permute-done.mine
  14.2 0.0 collective-permute-start.1
  14.2 0.4 %collective-permute-done.4.theirs = bf16[224,384]{1,0:T(8,128)(2,1)S(1)} collective-permute-done((bf16[224,384]{1,0:T(8,128)(2,1)S(1)}, bf16[224,384]{1,0:T(8,128)(2,1)S(1)}, u32[]{:S(2)}, u32[]{:S(2)}) %collective-permute-start.4) | collective-permute-done | bytes 172064 | tf_op jit(solution)/shard_map/ppermute | solution.py:239
  14.6 0.2 collective-permute-start.5
  14.8 3.0 %collective-permute-done.6.near = bf16[192,384]{1,0:T(8,128)(2,1)S(1)} collective-permute-done((bf16[192,384]{1,0:T(8,128)(2,1)S(1)}, bf16[192,384]{1,0:T(8,128)(2,1)S(1)}, u32[]{:S(2)}, u32[]{:S(2)}) %collective-permute-start.6) | collective-permute-done | bytes 147488 | tf_op jit(solution)/shard_map/ppermute | solution.py:222
  17.8 0.0 collective-permute-start.7
  17.8 1.4 %shard_map.37.acc = f32[384,1536]{1,0:T(8,128)S(1)} custom-call(bf16[4,384,384]{2,1,0:T(8,128)(2,1)S(1)} %bitcast.4, bf16[384,384]{1,0:T(8,128)(2,1)S(1)} %bitcast.10), custom_call_target="tpu_custom_call" | custom-call | flops 905969664 | bytes 1179648 | tf_op jit(solution)/shard_map/pallas_call | solution.py:236
  19.2 0.0 collective-permute-done.1.theirs
  19.2 1.4 %shard_map.39.acc = f32[384,1536]{1,0:T(8,128)S(1)} custom-call(f32[384,1536]{1,0:T(8,128)S(1)} %shard_map.37.acc, bf16[4,384,384]{2,1,0:T(8,128)(2,1)S(1)} %bitcast.5, bf16[192,384]{1,0:T(8,128)(2,1)S(1)} %collective-permute-done.mine, bf16[192,384]{1,0:T(8,128)(2,1)S(1)} %collective-permute-done.1.theirs), custom_call_target="tpu_custom_call", output_to_operand_aliasing={{}: (0, {})} | custom-call | flops 905969664 | bytes 1179648 | tf_op jit(solution)/shard_map/pallas_call | solution.py:256
  20.7 0.8 %shard_map.44.ahead = bf16[1536,768]{1,0:T(8,128)(2,1)S(1)} custom-call(bf16[4,384,384]{2,1,0:T(8,128)(2,1)S(1)} %bitcast.6, bf16[320,384]{1,0:T(8,128)(2,1)S(1)} %shard_map.43.packed, bf16[192,384]{1,0:T(8,128)(2,1)S(1)} %collective-permute-done.6.near), custom_call_target="tpu_custom_call" | custom-call | flops 452984832 | bytes 1179648 | tf_op jit(solution)/shard_map/pallas_call | solution.py:265
  21.5 0.0 collective-permute-done.7.swapped
  21.5 0.0 collective-permute-done.5.other
  21.5 2.9 %shard_map.45 = (bf16[4,384,384]{2,1,0:T(8,128)(2,1)}, bf16[1536,768]{1,0:T(8,128)(2,1)S(1)}) custom-call(f32[384,1536]{1,0:T(8,128)S(1)} %shard_map.39.acc, bf16[4,384,384]{2,1,0:T(8,128)(2,1)S(1)} %bitcast.7, bf16[320,384]{1,0:T(8,128)(2,1)S(1)} %shard_map.43.packed, ...), custom_call_target="tpu_custom_call", output_to_operand_aliasing={{1}: (7, {})} | custom-call | flops 1358954496 | bytes 2359296 | tf_op jit(solution)/shard_map/pallas_call | solution.py:272
  (3 shorter events, 0.1 us)
Async XLA Ops:
  0.0 5.1 %copy-start.1 = (bf16[16,384,128]{2,1,0:T(8,128)(2,1)S(1)}, bf16[16,384,128]{2,1,0:T(8,128)(2,1)}, u32[]{:S(2)}) copy-start(bf16[16,384,128]{2,1,0:T(8,128)(2,1)} %u.3) | copy-start | bytes 4718596
  0.0 5.1 %copy-start = (bf16[1,4,384,384]{3,2,1,0:T(8,128)(2,1)S(1)}, bf16[1,4,384,384]{3,2,1,0:T(8,128)(2,1)}, u32[]{:S(2)}) copy-start(bf16[1,4,384,384]{3,2,1,0:T(8,128)(2,1)} %param.3) | copy-start | bytes 3538948
  0.0 5.7 %copy-start.2 = (bf16[1,384,384]{2,1,0:T(8,128)(2,1)S(1)}, bf16[1,384,384]{2,1,0:T(8,128)(2,1)}, u32[]{:S(2)}) copy-start(bf16[1,384,384]{2,1,0:T(8,128)(2,1)} %param.4) | copy-start | bytes 884740
  1.0 8.1 %collective-permute-start.3 = (bf16[96,384]{1,0:T(8,128)(2,1)S(1)}, bf16[96,384]{1,0:T(8,128)(2,1)S(1)}, u32[]{:S(2)}, u32[]{:S(2)}) collective-permute-start(bf16[96,384]{1,0:T(8,128)(2,1)S(1)} %shard_map.41), channel_id=1, source_target_pairs={{0,8},{4,12},{8,0},{12,4},{1,9},{5,13},{9,1},{13,5},{2,10},{6,14},... | collective-permute-start | bytes 221192 | tf_op jit(solution)/shard_map/ppermute | solution.py:211
  5.6 3.5 %collective-permute-start.2 = (f32[384,128]{1,0:T(8,128)S(1)}, f32[384,128]{1,0:T(8,128)S(1)}, u32[]{:S(2)}, u32[]{:S(2)}) collective-permute-start(f32[384,128]{1,0:T(8,128)S(1)} %shard_map.40.part), channel_id=1, source_target_pairs={{0,1},{1,0},{2,3},{3,2},{4,5},{5,4},{6,7},{7,6},{8,9},{9,8},{10,11... | collective-permute-start | bytes 589832 | tf_op jit(solution)/shard_map/ppermute | solution.py:231
  5.7 8.5 %collective-permute-start = (bf16[192,384]{1,0:T(8,128)(2,1)S(1)}, bf16[192,384]{1,0:T(8,128)(2,1)S(1)}, u32[]{:S(2)}, u32[]{:S(2)}) collective-permute-start(bf16[192,384]{1,0:T(8,128)(2,1)S(1)} %shard_map.38), channel_id=1, source_target_pairs={{0,4},{4,0},{8,12},{12,8},{1,5},{5,1},{9,13},{13,9},{2,6},{6,2},{1... | collective-permute-start | bytes 442376 | tf_op jit(solution)/shard_map/ppermute | solution.py:222
  9.1 5.5 %collective-permute-start.4 = (bf16[224,384]{1,0:T(8,128)(2,1)S(1)}, bf16[224,384]{1,0:T(8,128)(2,1)S(1)}, u32[]{:S(2)}, u32[]{:S(2)}) collective-permute-start(bf16[224,384]{1,0:T(8,128)(2,1)S(1)} %shard_map.42.mine), channel_id=1, source_target_pairs={{0,2},{1,17},{2,0},{3,19},{16,18},{17,1},{18,16},{19,3},{4,6},{5,2... | collective-permute-start | bytes 516104 | tf_op jit(solution)/shard_map/ppermute | solution.py:239
  10.9 6.9 %collective-permute-start.6 = (bf16[192,384]{1,0:T(8,128)(2,1)S(1)}, bf16[192,384]{1,0:T(8,128)(2,1)S(1)}, u32[]{:S(2)}, u32[]{:S(2)}) collective-permute-start(bf16[192,384]{1,0:T(8,128)(2,1)S(1)} %shard_map.38), channel_id=1, source_target_pairs={{0,12},{4,8},{8,4},{12,0},{1,13},{5,9},{9,5},{13,1},{2,14},{6,10},... | collective-permute-start | bytes 442376 | tf_op jit(solution)/shard_map/ppermute | solution.py:222
  14.2 5.0 %collective-permute-start.1 = (bf16[192,384]{1,0:T(8,128)(2,1)S(1)}, bf16[192,384]{1,0:T(8,128)(2,1)S(1)}, u32[]{:S(2)}, u32[]{:S(2)}) collective-permute-start(bf16[192,384]{1,0:T(8,128)(2,1)S(1)} %collective-permute-done.mine), channel_id=1, source_target_pairs={{0,1},{1,0},{2,3},{3,2},{4,5},{5,4},{6,7},{7,6},{8,9},{9,8},{10,11... | collective-permute-start | bytes 442376 | tf_op jit(solution)/shard_map/ppermute | solution.py:253
  14.6 6.9 %collective-permute-start.5 = (bf16[320,384]{1,0:T(8,128)(2,1)S(1)}, bf16[320,384]{1,0:T(8,128)(2,1)S(1)}, u32[]{:S(2)}, u32[]{:S(2)}) collective-permute-start(bf16[320,384]{1,0:T(8,128)(2,1)S(1)} %shard_map.43.packed), channel_id=1, source_target_pairs={{0,1},{1,0},{2,3},{3,2},{4,5},{5,4},{6,7},{7,6},{8,9},{9,8},{10,11... | collective-permute-start | bytes 737288 | tf_op jit(solution)/shard_map/ppermute | solution.py:249
  17.8 3.7 %collective-permute-start.7 = (bf16[192,384]{1,0:T(8,128)(2,1)S(1)}, bf16[192,384]{1,0:T(8,128)(2,1)S(1)}, u32[]{:S(2)}, u32[]{:S(2)}) collective-permute-start(bf16[192,384]{1,0:T(8,128)(2,1)S(1)} %collective-permute-done.6.near), channel_id=1, source_target_pairs={{0,1},{1,0},{2,3},{3,2},{4,5},{5,4},{6,7},{7,6},{8,9},{9,8},{10,11... | collective-permute-start | bytes 442376 | tf_op jit(solution)/shard_map/ppermute | solution.py:253

commit v5 on v4

--- a/solution.py
+++ b/solution.py
@@ -40,18 +40,13 @@
 
 
 def take_far(index_of, src, out, sems):
-    rows = out.shape[0] // 3
-    start = index_of() * out.shape[0]
-    copies = [
-        pltpu.make_async_copy(
-            src.at[pl.ds(pl.multiple_of(start + k * rows, rows), rows), :],
-            out.at[pl.ds(k * rows, rows), :],
-            sems.at[k],
-        )
-        for k in range(3)
-    ]
-    for copy in copies:
-        copy.start()
+    count = sems.shape[0]
+    rows = out.shape[0] // count
+    copies = []
+    for k in range(count):
+        at = pl.multiple_of((index_of() * count + k) * rows, rows)
+        copies.append(pltpu.make_async_copy(src.at[pl.ds(at, rows), :], out.at[pl.ds(k * rows, rows), :], sems.at[k]))
+        copies[-1].start()
     for copy in copies:
         copy.wait()
 
@@ -168,7 +163,7 @@
         copy.wait()
 
 
-def sigma_block(n_i, n_j, doubles, aux_factors, cycle_factors):
+def sigma_block(n_g, n_i, n_j, doubles, aux_factors, cycle_factors):
     rows_i, cols_j, width, _ = doubles.shape
     pairs = rows_i * cols_j
     rank = cycle_factors.shape[-1]
@@ -176,7 +171,7 @@
     own = aux_factors.reshape(width, width)
     quarter, half = width // 4, width // 2
     fold = rank
-    assert width % rank == 0 and fold * (width // rank) == width
+    assert width % rank == 0 and pairs % 2 == 0 and n_g % 2 == 0 and n_j % 4 == 0
     flops = 2 * pairs * width * width * width
     moved = 2 * pairs * width * width
 
@@ -196,7 +191,7 @@
 
     core_swap = [(j, j ^ 1) for j in range(n_j)]
     chip_swap = [
-        (g * n_j + j, (g ^ 1) * n_j + j if j % 2 else g * n_j + (j ^ 2)) for g in range(2) for j in range(n_j)
+        (g * n_j + j, (g ^ 1) * n_j + j if j % 2 else g * n_j + (j ^ 2)) for g in range(n_g) for j in range(n_j)
     ]
     far_away = n_i // 2
 
@@ -204,7 +199,7 @@
         functools.partial(take_far, quarter_of),
         pltpu.VMEM((quarter, width), BF16),
         [HBM],
-        [pltpu.SemaphoreType.DMA((3,))],
+        [pltpu.SemaphoreType.DMA((3 if quarter % 48 == 0 else 1,))],
         flops=2 * flops,
         moved=moved * 2 // 2,
     )(in_hbm(own))
@@ -287,11 +282,11 @@
 
 
 def solution(mesh):
-    n_i, n_j = mesh.shape["ia"], mesh.shape["ja"]
+    n_g, n_i, n_j = (mesh.shape[axis] for axis in ("grp", "ia", "ja"))
     in_specs = (P(("grp", "ia"), "ja", None, None), P("ia", None, None), P())
     out_specs = P(("grp", "ia"), "ja", None, None)
 
     def block(*args):
-        return sigma_block(n_i, n_j, *args)
+        return sigma_block(n_g, n_i, n_j, *args)
 
     return jax.shard_map(block, mesh=mesh, in_specs=in_specs, out_specs=out_specs, check_vma=False)

time: 24.6 us -> 24.6 us (level)
  no operation moved by 1% of the time
where the time goes in v5:
time: 24.6 us; the launch traced here: 24.4 us
  starting transfers between devices  11.2 us (46%)
  Pallas kernels  8.04 us (33%)
  waiting for transfers between devices  5.04 us (20%)
    ppermute x2, starting transfers between devices, sigma_block(): near[k] = lax.ppermute(rows, 'ia', [(i, across(i, k)) for i in range(n_i)])  4.97 us
    ppermute x1, starting transfers between devices, sigma_block(): lax.ppermute(piece, 'ia', [(i, across(i, far_away)) for i in range(n_i)])  4.15 us
    ppermute x2, waiting for transfers between devices, sigma_block(): near[k] = lax.ppermute(rows, 'ia', [(i, across(i, k)) for i in range(n_i)])  2.99 us
    pallas_call x1, Pallas kernels, sigma_block(): call(functools.partial(ladder_last, spot, first_j, quarter), (jax.ShapeDt...  2.88 us
    ppermute x1, starting transfers between devices, sigma_block(): other = lax.ppermute(packed, ('grp', 'ja'), chip_swap)  1.79 us
    ppermute x1, waiting for transfers between devices, sigma_block(): lax.ppermute(piece, 'ia', [(i, across(i, far_away)) for i in range(n_i)])  1.69 us
    pallas_call x1, Pallas kernels, sigma_block(): call(functools.partial(ladder_near, spot), wide, [VMEM] * 4, [whole, half...  1.43 us
    pallas_call x1, Pallas kernels, sigma_block(): call(ladder_first, wide, [VMEM] * 2, [halfway], flops=2 * flops, moved=mo...  1.41 us
  transfers between devices with their start and end apart: 8, of which 3 were waited for; matrix products, arithmetic and copies ran while one was open for 0% of the time, Pallas kernels for 17%

profile of v5, /device:TPU:0, one launch (start us, length us, event | category | flops | bytes accessed | tf_op | source)
XLA Modules:
  0.0 24.4 jit_solution(4627184525295371088)
XLA Ops:
  0.0 0.0 copy-start.1
  0.0 0.0 copy-start
  0.0 0.0 copy-start.2
  0.0 0.9 %shard_map.41 = bf16[96,384]{1,0:T(8,128)(2,1)S(1)} custom-call(bf16[384,384]{1,0:T(8,128)(2,1)} %bitcast.8), custom_call_target="tpu_custom_call" | custom-call | flops 905969664 | bytes 1179648 | tf_op jit(solution)/shard_map/pallas_call | solution.py:198
  1.0 4.2 %collective-permute-start.3 = (bf16[96,384]{1,0:T(8,128)(2,1)S(1)}, bf16[96,384]{1,0:T(8,128)(2,1)S(1)}, u32[]{:S(2)}, u32[]{:S(2)}) collective-permute-start(bf16[96,384]{1,0:T(8,128)(2,1)S(1)} %shard_map.41), channel_id=1, source_target_pairs={{0,8},{4,12},{8,0},{12,4},{1,9},{5,13},{9,1},{13,5},{2,10},{6,14},... | collective-permute-start | bytes 221192 | tf_op jit(solution)/shard_map/ppermute | solution.py:206
  5.1 0.0 copy-done.1
  5.1 0.0 copy-done
  5.1 0.5 %shard_map.40.part = f32[384,128]{1,0:T(8,128)S(1)} custom-call(bf16[4,384,384]{2,1,0:T(8,128)(2,1)S(1)} %bitcast.3, bf16[16,384,128]{2,1,0:T(8,128)(2,1)S(1)} %copy-done.1), custom_call_target="tpu_custom_call" | custom-call | flops 150994944 | bytes 1179648 | tf_op jit(solution)/shard_map/pallas_call | solution.py:219
  5.6 0.1 collective-permute-start.2
  5.7 0.0 copy-done.2
  5.7 1.6 %collective-permute-start = (bf16[192,384]{1,0:T(8,128)(2,1)S(1)}, bf16[192,384]{1,0:T(8,128)(2,1)S(1)}, u32[]{:S(2)}, u32[]{:S(2)}) collective-permute-start(bf16[192,384]{1,0:T(8,128)(2,1)S(1)} %shard_map.38), channel_id=1, source_target_pairs={{0,4},{4,0},{8,12},{12,8},{1,5},{5,1},{9,13},{13,9},{2,6},{6,2},{1... | collective-permute-start | bytes 442376 | tf_op jit(solution)/shard_map/ppermute | solution.py:217
  7.4 1.7 %collective-permute-done.3.piece = bf16[96,384]{1,0:T(8,128)(2,1)S(1)} collective-permute-done((bf16[96,384]{1,0:T(8,128)(2,1)S(1)}, bf16[96,384]{1,0:T(8,128)(2,1)S(1)}, u32[]{:S(2)}, u32[]{:S(2)}) %collective-permute-start.3) | collective-permute-done | bytes 73760 | tf_op jit(solution)/shard_map/ppermute | solution.py:206
  9.0 0.0 collective-permute-done.2.got
  9.1 1.8 %collective-permute-start.4 = (bf16[224,384]{1,0:T(8,128)(2,1)S(1)}, bf16[224,384]{1,0:T(8,128)(2,1)S(1)}, u32[]{:S(2)}, u32[]{:S(2)}) collective-permute-start(bf16[224,384]{1,0:T(8,128)(2,1)S(1)} %shard_map.42.mine), channel_id=1, source_target_pairs={{0,2},{1,17},{2,0},{3,19},{16,18},{17,1},{18,16},{19,3},{4,6},{5,2... | collective-permute-start | bytes 516104 | tf_op jit(solution)/shard_map/ppermute | solution.py:234
  10.9 3.3 %collective-permute-start.6 = (bf16[192,384]{1,0:T(8,128)(2,1)S(1)}, bf16[192,384]{1,0:T(8,128)(2,1)S(1)}, u32[]{:S(2)}, u32[]{:S(2)}) collective-permute-start(bf16[192,384]{1,0:T(8,128)(2,1)S(1)} %shard_map.38), channel_id=1, source_target_pairs={{0,12},{4,8},{8,4},{12,0},{1,13},{5,9},{9,5},{13,1},{2,14},{6,10},... | collective-permute-start | bytes 442376 | tf_op jit(solution)/shard_map/ppermute | solution.py:217
  14.2 0.0 collective-permute-done.mine
  14.2 0.0 collective-permute-start.1
  14.2 0.4 %collective-permute-done.4.theirs = bf16[224,384]{1,0:T(8,128)(2,1)S(1)} collective-permute-done((bf16[224,384]{1,0:T(8,128)(2,1)S(1)}, bf16[224,384]{1,0:T(8,128)(2,1)S(1)}, u32[]{:S(2)}, u32[]{:S(2)}) %collective-permute-start.4) | collective-permute-done | bytes 172064 | tf_op jit(solution)/shard_map/ppermute | solution.py:234
  14.6 0.2 collective-permute-start.5
  14.8 3.0 %collective-permute-done.6.near = bf16[192,384]{1,0:T(8,128)(2,1)S(1)} collective-permute-done((bf16[192,384]{1,0:T(8,128)(2,1)S(1)}, bf16[192,384]{1,0:T(8,128)(2,1)S(1)}, u32[]{:S(2)}, u32[]{:S(2)}) %collective-permute-start.6) | collective-permute-done | bytes 147488 | tf_op jit(solution)/shard_map/ppermute | solution.py:217
  17.8 0.0 collective-permute-start.7
  17.8 1.4 %shard_map.37.acc = f32[384,1536]{1,0:T(8,128)S(1)} custom-call(bf16[4,384,384]{2,1,0:T(8,128)(2,1)S(1)} %bitcast.4, bf16[384,384]{1,0:T(8,128)(2,1)S(1)} %bitcast.10), custom_call_target="tpu_custom_call" | custom-call | flops 905969664 | bytes 1179648 | tf_op jit(solution)/shard_map/pallas_call | solution.py:231
  19.2 0.0 collective-permute-done.1.theirs
  19.2 1.4 %shard_map.39.acc = f32[384,1536]{1,0:T(8,128)S(1)} custom-call(f32[384,1536]{1,0:T(8,128)S(1)} %shard_map.37.acc, bf16[4,384,384]{2,1,0:T(8,128)(2,1)S(1)} %bitcast.5, bf16[192,384]{1,0:T(8,128)(2,1)S(1)} %collective-permute-done.mine, bf16[192,384]{1,0:T(8,128)(2,1)S(1)} %collective-permute-done.1.theirs), custom_call_target="tpu_custom_call", output_to_operand_aliasing={{}: (0, {})} | custom-call | flops 905969664 | bytes 1179648 | tf_op jit(solution)/shard_map/pallas_call | solution.py:251
  20.7 0.8 %shard_map.44.ahead = bf16[1536,768]{1,0:T(8,128)(2,1)S(1)} custom-call(bf16[4,384,384]{2,1,0:T(8,128)(2,1)S(1)} %bitcast.6, bf16[320,384]{1,0:T(8,128)(2,1)S(1)} %shard_map.43.packed, bf16[192,384]{1,0:T(8,128)(2,1)S(1)} %collective-permute-done.6.near), custom_call_target="tpu_custom_call" | custom-call | flops 452984832 | bytes 1179648 | tf_op jit(solution)/shard_map/pallas_call | solution.py:260
  21.5 0.0 collective-permute-done.7.swapped
  21.5 0.0 collective-permute-done.5.other
  21.5 2.9 %shard_map.45 = (bf16[4,384,384]{2,1,0:T(8,128)(2,1)}, bf16[1536,768]{1,0:T(8,128)(2,1)S(1)}) custom-call(f32[384,1536]{1,0:T(8,128)S(1)} %shard_map.39.acc, bf16[4,384,384]{2,1,0:T(8,128)(2,1)S(1)} %bitcast.7, bf16[320,384]{1,0:T(8,128)(2,1)S(1)} %shard_map.43.packed, ...), custom_call_target="tpu_custom_call", output_to_operand_aliasing={{1}: (7, {})} | custom-call | flops 1358954496 | bytes 2359296 | tf_op jit(solution)/shard_map/pallas_call | solution.py:267
  (3 shorter events, 0.1 us)
Async XLA Ops:
  0.0 5.1 %copy-start.1 = (bf16[16,384,128]{2,1,0:T(8,128)(2,1)S(1)}, bf16[16,384,128]{2,1,0:T(8,128)(2,1)}, u32[]{:S(2)}) copy-start(bf16[16,384,128]{2,1,0:T(8,128)(2,1)} %u.3) | copy-start | bytes 4718596
  0.0 5.1 %copy-start = (bf16[1,4,384,384]{3,2,1,0:T(8,128)(2,1)S(1)}, bf16[1,4,384,384]{3,2,1,0:T(8,128)(2,1)}, u32[]{:S(2)}) copy-start(bf16[1,4,384,384]{3,2,1,0:T(8,128)(2,1)} %param.3) | copy-start | bytes 3538948
  0.0 5.7 %copy-start.2 = (bf16[1,384,384]{2,1,0:T(8,128)(2,1)S(1)}, bf16[1,384,384]{2,1,0:T(8,128)(2,1)}, u32[]{:S(2)}) copy-start(bf16[1,384,384]{2,1,0:T(8,128)(2,1)} %param.4) | copy-start | bytes 884740
  1.0 8.1 %collective-permute-start.3 = (bf16[96,384]{1,0:T(8,128)(2,1)S(1)}, bf16[96,384]{1,0:T(8,128)(2,1)S(1)}, u32[]{:S(2)}, u32[]{:S(2)}) collective-permute-start(bf16[96,384]{1,0:T(8,128)(2,1)S(1)} %shard_map.41), channel_id=1, source_target_pairs={{0,8},{4,12},{8,0},{12,4},{1,9},{5,13},{9,1},{13,5},{2,10},{6,14},... | collective-permute-start | bytes 221192 | tf_op jit(solution)/shard_map/ppermute | solution.py:206
  5.6 3.5 %collective-permute-start.2 = (f32[384,128]{1,0:T(8,128)S(1)}, f32[384,128]{1,0:T(8,128)S(1)}, u32[]{:S(2)}, u32[]{:S(2)}) collective-permute-start(f32[384,128]{1,0:T(8,128)S(1)} %shard_map.40.part), channel_id=1, source_target_pairs={{0,1},{1,0},{2,3},{3,2},{4,5},{5,4},{6,7},{7,6},{8,9},{9,8},{10,11... | collective-permute-start | bytes 589832 | tf_op jit(solution)/shard_map/ppermute | solution.py:226
  5.7 8.5 %collective-permute-start = (bf16[192,384]{1,0:T(8,128)(2,1)S(1)}, bf16[192,384]{1,0:T(8,128)(2,1)S(1)}, u32[]{:S(2)}, u32[]{:S(2)}) collective-permute-start(bf16[192,384]{1,0:T(8,128)(2,1)S(1)} %shard_map.38), channel_id=1, source_target_pairs={{0,4},{4,0},{8,12},{12,8},{1,5},{5,1},{9,13},{13,9},{2,6},{6,2},{1... | collective-permute-start | bytes 442376 | tf_op jit(solution)/shard_map/ppermute | solution.py:217
  9.1 5.5 %collective-permute-start.4 = (bf16[224,384]{1,0:T(8,128)(2,1)S(1)}, bf16[224,384]{1,0:T(8,128)(2,1)S(1)}, u32[]{:S(2)}, u32[]{:S(2)}) collective-permute-start(bf16[224,384]{1,0:T(8,128)(2,1)S(1)} %shard_map.42.mine), channel_id=1, source_target_pairs={{0,2},{1,17},{2,0},{3,19},{16,18},{17,1},{18,16},{19,3},{4,6},{5,2... | collective-permute-start | bytes 516104 | tf_op jit(solution)/shard_map/ppermute | solution.py:234
  10.9 6.9 %collective-permute-start.6 = (bf16[192,384]{1,0:T(8,128)(2,1)S(1)}, bf16[192,384]{1,0:T(8,128)(2,1)S(1)}, u32[]{:S(2)}, u32[]{:S(2)}) collective-permute-start(bf16[192,384]{1,0:T(8,128)(2,1)S(1)} %shard_map.38), channel_id=1, source_target_pairs={{0,12},{4,8},{8,4},{12,0},{1,13},{5,9},{9,5},{13,1},{2,14},{6,10},... | collective-permute-start | bytes 442376 | tf_op jit(solution)/shard_map/ppermute | solution.py:217
  14.2 5.0 %collective-permute-start.1 = (bf16[192,384]{1,0:T(8,128)(2,1)S(1)}, bf16[192,384]{1,0:T(8,128)(2,1)S(1)}, u32[]{:S(2)}, u32[]{:S(2)}) collective-permute-start(bf16[192,384]{1,0:T(8,128)(2,1)S(1)} %collective-permute-done.mine), channel_id=1, source_target_pairs={{0,1},{1,0},{2,3},{3,2},{4,5},{5,4},{6,7},{7,6},{8,9},{9,8},{10,11... | collective-permute-start | bytes 442376 | tf_op jit(solution)/shard_map/ppermute | solution.py:248
  14.6 6.9 %collective-permute-start.5 = (bf16[320,384]{1,0:T(8,128)(2,1)S(1)}, bf16[320,384]{1,0:T(8,128)(2,1)S(1)}, u32[]{:S(2)}, u32[]{:S(2)}) collective-permute-start(bf16[320,384]{1,0:T(8,128)(2,1)S(1)} %shard_map.43.packed), channel_id=1, source_target_pairs={{0,1},{1,0},{2,3},{3,2},{4,5},{5,4},{6,7},{7,6},{8,9},{9,8},{10,11... | collective-permute-start | bytes 737288 | tf_op jit(solution)/shard_map/ppermute | solution.py:244
  17.8 3.7 %collective-permute-start.7 = (bf16[192,384]{1,0:T(8,128)(2,1)S(1)}, bf16[192,384]{1,0:T(8,128)(2,1)S(1)}, u32[]{:S(2)}, u32[]{:S(2)}) collective-permute-start(bf16[192,384]{1,0:T(8,128)(2,1)S(1)} %collective-permute-done.6.near), channel_id=1, source_target_pairs={{0,1},{1,0},{2,3},{3,2},{4,5},{5,4},{6,7},{7,6},{8,9},{9,8},{10,11... | collective-permute-start | bytes 442376 | tf_op jit(solution)/shard_map/ppermute | solution.py:248

commit v6 on v5

--- a/solution.py
+++ b/solution.py
@@ -106,18 +106,23 @@
     out[2 * rows :] = (mine[rows:].astype(F32) + theirs[rows:].astype(F32)).astype(BF16)
 
 
-def first_products(r, pieces, halfway):
+def first_products(r, pieces):
     n, width, _ = r.shape
     stack = jnp.concatenate([rows for rows, _, _ in pieces], 0)
-    for g in range(0, n, 2):
-        h = mm_nt(stack, r[g : g + 2].reshape(2 * width, width)).astype(BF16)
-        top = 0
-        for rows, p, start in pieces:
-            size = rows.shape[0]
-            for k in range(2):
-                at = pl.multiple_of((g + k) * width + start, size)
-                halfway[pl.ds(at, size), p * width : (p + 1) * width] = h[top : top + size, k * width : (k + 1) * width]
-            top += size
+    return mm_nt(stack, r[...].reshape(n * width, width)).astype(BF16)
+
+
+def spread(products, pieces, halfway):
+    width = halfway.shape[1] // 2
+    top = 0
+    for rows, p, start in pieces:
+        size = rows.shape[0]
+        for q in range(halfway.shape[0] // width):
+            at = pl.multiple_of(q * width + start, size)
+            halfway[pl.ds(at, size), p * width : (p + 1) * width] = products[
+                top : top + size, q * width : (q + 1) * width
+            ]
+        top += size
 
 
 def held_rows(spot, rows, which, packed, near):
@@ -130,8 +135,8 @@
     ]
 
 
-def ladder_ahead(spot, rows, r, packed, near, halfway):
-    first_products(r, held_rows(spot, rows, spot()[1], packed, near), halfway)
+def ladder_ahead(spot, rows, r, packed, near, out):
+    out[...] = first_products(r, held_rows(spot, rows, spot()[1], packed, near))
 
 
 def ladder_last(
@@ -139,9 +144,11 @@
 ):
     n, width, _ = r.shape
     core = spot()[1]
+    ours = held_rows(spot, rows, core, packed, near)
     theirs = held_rows(spot, rows, 1 - core, other, swapped)
-    first_products(r, theirs, halfway)
-    for piece, p, start in held_rows(spot, rows, core, packed, near) + theirs:
+    spread(ahead, ours, halfway)
+    spread(first_products(r, theirs), theirs, halfway)
+    for piece, p, start in ours + theirs:
         size = piece.shape[0]
         wide[pl.ds(pl.multiple_of(start, size), size), p * width : (p + 1) * width] = piece
     folded = jnp.where(core == 0, packed[2 * rows :], other[2 * rows :])
@@ -259,22 +266,22 @@
         )(acc, r, near[k], swapped[k])
     ahead = call(
         functools.partial(ladder_ahead, spot, quarter),
-        pltpu.VMEM((pairs * width, 2 * width), BF16),
+        pltpu.VMEM((2 * half, pairs * width), BF16),
         [VMEM] * 3,
         flops=flops,
         moved=moved,
     )(r, packed, near[last])
-    out, _ = call(
+    out = call(
         functools.partial(ladder_last, spot, first_j, quarter),
-        (jax.ShapeDtypeStruct((pairs, width, width), BF16), pltpu.VMEM((pairs * width, 2 * width), BF16)),
+        jax.ShapeDtypeStruct((pairs, width, width), BF16),
         [VMEM] * 8,
         [
+            pltpu.VMEM((pairs * width, 2 * width), BF16),
             pltpu.VMEM((width, 2 * width), BF16),
             pltpu.VMEM((width, rank), BF16),
             pltpu.VMEM((pairs, width, width), BF16),
             pltpu.SemaphoreType.DMA((pairs,)),
         ],
-        {7: 1},
         flops=3 * flops,
         moved=2 * moved,
     )(acc, r, packed, other, near[last], swapped[last], cycle_factors, ahead)

time: 24.6 us -> 29.4 us (1.20)
  local copies, waits for them, and re-layouts: 0.01 us -> 3.26 us
  waiting for transfers between devices: 5.04 us -> 6.29 us
    unnamed x6 -> x10, local copies, waits for them, and re-layouts: 0.01 us -> 3.26 us
    ppermute x1, waiting for transfers between devices: 1.69 us -> 2.79 us  [sigma_block(): lax.ppermute(piece, 'ia', [(i, across(i, far_away)) for i in range(n_i)])]
    ppermute x1, starting transfers between devices: 0.07 us -> 0.56 us  [sigma_block(): got = lax.ppermute(part, 'ja', core_swap)]
    ppermute x1, starting transfers between devices: 4.15 us -> 3.67 us  [sigma_block(): lax.ppermute(piece, 'ia', [(i, across(i, far_away)) for i in range(n_i)])]
  transfers between devices with their start and end apart: 8 -> 8, of which waited for: 3 -> 3; matrix products, arithmetic and copies ran while one was open for 0% -> 0% of each run, Pallas kernels for 17% -> 16%
where the time goes in v6:
time: 29.4 us; the launch traced here: 29.2 us
  starting transfers between devices  11.4 us (39%)
  Pallas kernels  8.09 us (28%)
  waiting for transfers between devices  6.29 us (21%)
  local copies, waits for them, and re-layouts  3.26 us (11%)
    ppermute x2, starting transfers between devices, sigma_block(): near[k] = lax.ppermute(rows, 'ia', [(i, across(i, k)) for i in range(n_i)])  5.13 us
    ppermute x1, starting transfers between devices, sigma_block(): lax.ppermute(piece, 'ia', [(i, across(i, far_away)) for i in range(n_i)])  3.67 us
    unnamed x10, local copies, waits for them, and re-layouts  3.26 us
    ppermute x2, waiting for transfers between devices, sigma_block(): near[k] = lax.ppermute(rows, 'ia', [(i, across(i, k)) for i in range(n_i)])  3.25 us
    pallas_call x1, Pallas kernels, sigma_block(): call(functools.partial(ladder_last, spot, first_j, quarter), jax.ShapeDty...  3.02 us
    ppermute x1, waiting for transfers between devices, sigma_block(): lax.ppermute(piece, 'ia', [(i, across(i, far_away)) for i in range(n_i)])  2.79 us
    ppermute x1, starting transfers between devices, sigma_block(): other = lax.ppermute(packed, ('grp', 'ja'), chip_swap)  1.73 us
    pallas_call x1, Pallas kernels, sigma_block(): call(functools.partial(ladder_near, spot), wide, [VMEM] * 4, [whole, half...  1.44 us
  transfers between devices with their start and end apart: 8, of which 3 were waited for; matrix products, arithmetic and copies ran while one was open for 0% of the time, Pallas kernels for 16%

profile of v6, /device:TPU:0, one launch (start us, length us, event | category | flops | bytes accessed | tf_op | source)
XLA Modules:
  0.0 29.2 jit_solution(9771776889246794152)
XLA Ops:
  0.0 0.0 copy-start
  0.0 1.3 %copy-done = bf16[1,4,384,384]{3,2,1,0:T(8,128)(2,1)S(1)} copy-done((bf16[1,4,384,384]{3,2,1,0:T(8,128)(2,1)S(1)}, bf16[1,4,384,384]{3,2,1,0:T(8,128)(2,1)}, u32[]{:S(2)}) %copy-start) | copy-done | bytes 1179672
  1.3 0.0 copy-start.2
  1.3 1.4 %copy-done.2 = bf16[16,384,128]{2,1,0:T(8,128)(2,1)S(1)} copy-done((bf16[16,384,128]{2,1,0:T(8,128)(2,1)S(1)}, bf16[16,384,128]{2,1,0:T(8,128)(2,1)}, u32[]{:S(2)}) %copy-start.2) | copy-done | bytes 1572888
  2.7 0.5 %shard_map.40.part = f32[384,128]{1,0:T(8,128)S(1)} custom-call(bf16[4,384,384]{2,1,0:T(8,128)(2,1)S(1)} %bitcast.3, bf16[16,384,128]{2,1,0:T(8,128)(2,1)S(1)} %copy-done.2), custom_call_target="tpu_custom_call" | custom-call | flops 150994944 | bytes 1179648 | tf_op jit(solution)/shard_map/pallas_call | solution.py:226
  3.2 0.6 %collective-permute-start.2 = (f32[384,128]{1,0:T(8,128)S(1)}, f32[384,128]{1,0:T(8,128)S(1)}, u32[]{:S(2)}, u32[]{:S(2)}) collective-permute-start(f32[384,128]{1,0:T(8,128)S(1)} %shard_map.40.part), channel_id=1, source_target_pairs={{0,1},{1,0},{2,3},{3,2},{4,5},{5,4},{6,7},{7,6},{8,9},{9,8},{10,11... | collective-permute-start | bytes 589832 | tf_op jit(solution)/shard_map/ppermute | solution.py:233
  3.7 0.0 copy-start.4
  3.7 0.8 %shard_map.41 = bf16[96,384]{1,0:T(8,128)(2,1)S(1)} custom-call(bf16[384,384]{1,0:T(8,128)(2,1)} %bitcast.8), custom_call_target="tpu_custom_call" | custom-call | flops 905969664 | bytes 1179648 | tf_op jit(solution)/shard_map/pallas_call | solution.py:205
  4.6 3.7 %collective-permute-start.3 = (bf16[96,384]{1,0:T(8,128)(2,1)S(1)}, bf16[96,384]{1,0:T(8,128)(2,1)S(1)}, u32[]{:S(2)}, u32[]{:S(2)}) collective-permute-start(bf16[96,384]{1,0:T(8,128)(2,1)S(1)} %shard_map.41), channel_id=1, source_target_pairs={{0,8},{4,12},{8,0},{12,4},{1,9},{5,13},{9,1},{13,5},{2,10},{6,14},... | collective-permute-start | bytes 221192 | tf_op jit(solution)/shard_map/ppermute | solution.py:213
  8.2 0.0 copy-done.4
  8.3 0.0 copy-start.1
  8.3 1.6 %collective-permute-start = (bf16[192,384]{1,0:T(8,128)(2,1)S(1)}, bf16[192,384]{1,0:T(8,128)(2,1)S(1)}, u32[]{:S(2)}, u32[]{:S(2)}) collective-permute-start(bf16[192,384]{1,0:T(8,128)(2,1)S(1)} %shard_map.38), channel_id=1, source_target_pairs={{0,4},{4,0},{8,12},{12,8},{1,5},{5,1},{9,13},{13,9},{2,6},{6,2},{1... | collective-permute-start | bytes 442376 | tf_op jit(solution)/shard_map/ppermute | solution.py:224
  9.9 2.8 %collective-permute-done.3.piece = bf16[96,384]{1,0:T(8,128)(2,1)S(1)} collective-permute-done((bf16[96,384]{1,0:T(8,128)(2,1)S(1)}, bf16[96,384]{1,0:T(8,128)(2,1)S(1)}, u32[]{:S(2)}, u32[]{:S(2)}) %collective-permute-start.3) | collective-permute-done | bytes 73760 | tf_op jit(solution)/shard_map/ppermute | solution.py:213
  12.7 0.0 collective-permute-done.2.got
  12.7 1.7 %collective-permute-start.4 = (bf16[224,384]{1,0:T(8,128)(2,1)S(1)}, bf16[224,384]{1,0:T(8,128)(2,1)S(1)}, u32[]{:S(2)}, u32[]{:S(2)}) collective-permute-start(bf16[224,384]{1,0:T(8,128)(2,1)S(1)} %shard_map.42.mine), channel_id=1, source_target_pairs={{0,2},{1,17},{2,0},{3,19},{16,18},{17,1},{18,16},{19,3},{4,6},{5,2... | collective-permute-start | bytes 516104 | tf_op jit(solution)/shard_map/ppermute | solution.py:241
  14.5 3.5 %collective-permute-start.6 = (bf16[192,384]{1,0:T(8,128)(2,1)S(1)}, bf16[192,384]{1,0:T(8,128)(2,1)S(1)}, u32[]{:S(2)}, u32[]{:S(2)}) collective-permute-start(bf16[192,384]{1,0:T(8,128)(2,1)S(1)} %shard_map.38), channel_id=1, source_target_pairs={{0,12},{4,8},{8,4},{12,0},{1,13},{5,9},{9,5},{13,1},{2,14},{6,10},... | collective-permute-start | bytes 442376 | tf_op jit(solution)/shard_map/ppermute | solution.py:224
  18.0 0.0 collective-permute-done.mine
  18.0 0.0 collective-permute-start.1
  18.0 0.2 collective-permute-done.4.theirs
  18.3 0.3 %collective-permute-start.5 = (bf16[320,384]{1,0:T(8,128)(2,1)S(1)}, bf16[320,384]{1,0:T(8,128)(2,1)S(1)}, u32[]{:S(2)}, u32[]{:S(2)}) collective-permute-start(bf16[320,384]{1,0:T(8,128)(2,1)S(1)} %shard_map.43.packed), channel_id=1, source_target_pairs={{0,1},{1,0},{2,3},{3,2},{4,5},{5,4},{6,7},{7,6},{8,9},{9,8},{10,11... | collective-permute-start | bytes 737288 | tf_op jit(solution)/shard_map/ppermute | solution.py:251
  18.6 3.2 %collective-permute-done.6.near = bf16[192,384]{1,0:T(8,128)(2,1)S(1)} collective-permute-done((bf16[192,384]{1,0:T(8,128)(2,1)S(1)}, bf16[192,384]{1,0:T(8,128)(2,1)S(1)}, u32[]{:S(2)}, u32[]{:S(2)}) %collective-permute-start.6) | collective-permute-done | bytes 147488 | tf_op jit(solution)/shard_map/ppermute | solution.py:224
  21.8 0.0 collective-permute-start.7
  21.8 0.0 copy-done.1
  21.8 1.4 %shard_map.37.acc = f32[384,1536]{1,0:T(8,128)S(1)} custom-call(bf16[4,384,384]{2,1,0:T(8,128)(2,1)S(1)} %bitcast.4, bf16[384,384]{1,0:T(8,128)(2,1)S(1)} %bitcast.10), custom_call_target="tpu_custom_call" | custom-call | flops 905969664 | bytes 1179648 | tf_op jit(solution)/shard_map/pallas_call | solution.py:238
  23.3 0.0 collective-permute-done.1.theirs
  23.3 1.4 %shard_map.39.acc = f32[384,1536]{1,0:T(8,128)S(1)} custom-call(f32[384,1536]{1,0:T(8,128)S(1)} %shard_map.37.acc, bf16[4,384,384]{2,1,0:T(8,128)(2,1)S(1)} %bitcast.5, bf16[192,384]{1,0:T(8,128)(2,1)S(1)} %collective-permute-done.mine, bf16[192,384]{1,0:T(8,128)(2,1)S(1)} %collective-permute-done.1.theirs), custom_call_target="tpu_custom_call", output_to_operand_aliasing={{}: (0, {})} | custom-call | flops 905969664 | bytes 1179648 | tf_op jit(solution)/shard_map/pallas_call | solution.py:258
  24.7 0.0 copy-start.3
  24.7 0.8 %shard_map.44.ahead = bf16[384,1536]{1,0:T(8,128)(2,1)S(1)} custom-call(bf16[4,384,384]{2,1,0:T(8,128)(2,1)S(1)} %bitcast.6, bf16[320,384]{1,0:T(8,128)(2,1)S(1)} %shard_map.43.packed, bf16[192,384]{1,0:T(8,128)(2,1)S(1)} %collective-permute-done.6.near), custom_call_target="tpu_custom_call" | custom-call | flops 452984832 | bytes 1179648 | tf_op jit(solution)/shard_map/pallas_call | solution.py:267
  25.6 0.0 collective-permute-done.7.swapped
  25.6 0.0 collective-permute-done.5.other
  25.6 0.6 %copy-done.3 = bf16[16,384,128]{2,1,0:T(8,128)(2,1)S(1)} copy-done((bf16[16,384,128]{2,1,0:T(8,128)(2,1)S(1)}, bf16[16,384,128]{2,1,0:T(8,128)(2,1)}, u32[]{:S(2)}) %copy-start.3) | copy-done | bytes 1572888
  26.1 3.0 %shard_map.45 = bf16[4,384,384]{2,1,0:T(8,128)(2,1)} custom-call(f32[384,1536]{1,0:T(8,128)S(1)} %shard_map.39.acc, bf16[4,384,384]{2,1,0:T(8,128)(2,1)S(1)} %bitcast.7, bf16[320,384]{1,0:T(8,128)(2,1)S(1)} %shard_map.43.packed, bf16[320,384]{1,0:T(8,128)(2,1)S(1)} %collective-permute-done.5.other, bf16[192,384]{1,0:T(8,128)(2,1)S(1)} %collective-permute-done.6.near, ...), custom_call_target="tpu_custom_call" | custom-call | flops 1358954496 | bytes 2359296 | tf_op jit(solution)/shard_map/pallas_call | solution.py:274
  (3 shorter events, 0.1 us)
Async XLA Ops:
  0.0 1.3 %copy-start = (bf16[1,4,384,384]{3,2,1,0:T(8,128)(2,1)S(1)}, bf16[1,4,384,384]{3,2,1,0:T(8,128)(2,1)}, u32[]{:S(2)}) copy-start(bf16[1,4,384,384]{3,2,1,0:T(8,128)(2,1)} %param.3) | copy-start | bytes 3538948
  1.3 1.4 %copy-start.2 = (bf16[16,384,128]{2,1,0:T(8,128)(2,1)S(1)}, bf16[16,384,128]{2,1,0:T(8,128)(2,1)}, u32[]{:S(2)}) copy-start(bf16[16,384,128]{2,1,0:T(8,128)(2,1)} %u.3) | copy-start | bytes 4718596
  3.2 9.5 %collective-permute-start.2 = (f32[384,128]{1,0:T(8,128)S(1)}, f32[384,128]{1,0:T(8,128)S(1)}, u32[]{:S(2)}, u32[]{:S(2)}) collective-permute-start(f32[384,128]{1,0:T(8,128)S(1)} %shard_map.40.part), channel_id=1, source_target_pairs={{0,1},{1,0},{2,3},{3,2},{4,5},{5,4},{6,7},{7,6},{8,9},{9,8},{10,11... | collective-permute-start | bytes 589832 | tf_op jit(solution)/shard_map/ppermute | solution.py:233
  3.7 4.5 %copy-start.4 = (bf16[1,384,384]{2,1,0:T(8,128)(2,1)S(1)}, bf16[1,384,384]{2,1,0:T(8,128)(2,1)}, u32[]{:S(2)}) copy-start(bf16[1,384,384]{2,1,0:T(8,128)(2,1)} %param.4) | copy-start | bytes 884740
  4.6 8.1 %collective-permute-start.3 = (bf16[96,384]{1,0:T(8,128)(2,1)S(1)}, bf16[96,384]{1,0:T(8,128)(2,1)S(1)}, u32[]{:S(2)}, u32[]{:S(2)}) collective-permute-start(bf16[96,384]{1,0:T(8,128)(2,1)S(1)} %shard_map.41), channel_id=1, source_target_pairs={{0,8},{4,12},{8,0},{12,4},{1,9},{5,13},{9,1},{13,5},{2,10},{6,14},... | collective-permute-start | bytes 221192 | tf_op jit(solution)/shard_map/ppermute | solution.py:213
  8.3 13.6 %copy-start.1 = (bf16[1,4,384,384]{3,2,1,0:T(8,128)(2,1)S(1)}, bf16[1,4,384,384]{3,2,1,0:T(8,128)(2,1)}, u32[]{:S(2)}) copy-start(bf16[1,4,384,384]{3,2,1,0:T(8,128)(2,1)} %param.3) | copy-start | bytes 3538948
  8.3 9.7 %collective-permute-start = (bf16[192,384]{1,0:T(8,128)(2,1)S(1)}, bf16[192,384]{1,0:T(8,128)(2,1)S(1)}, u32[]{:S(2)}, u32[]{:S(2)}) collective-permute-start(bf16[192,384]{1,0:T(8,128)(2,1)S(1)} %shard_map.38), channel_id=1, source_target_pairs={{0,4},{4,0},{8,12},{12,8},{1,5},{5,1},{9,13},{13,9},{2,6},{6,2},{1... | collective-permute-start | bytes 442376 | tf_op jit(solution)/shard_map/ppermute | solution.py:224
  12.7 5.5 %collective-permute-start.4 = (bf16[224,384]{1,0:T(8,128)(2,1)S(1)}, bf16[224,384]{1,0:T(8,128)(2,1)S(1)}, u32[]{:S(2)}, u32[]{:S(2)}) collective-permute-start(bf16[224,384]{1,0:T(8,128)(2,1)S(1)} %shard_map.42.mine), channel_id=1, source_target_pairs={{0,2},{1,17},{2,0},{3,19},{16,18},{17,1},{18,16},{19,3},{4,6},{5,2... | collective-permute-start | bytes 516104 | tf_op jit(solution)/shard_map/ppermute | solution.py:241
  14.5 7.4 %collective-permute-start.6 = (bf16[192,384]{1,0:T(8,128)(2,1)S(1)}, bf16[192,384]{1,0:T(8,128)(2,1)S(1)}, u32[]{:S(2)}, u32[]{:S(2)}) collective-permute-start(bf16[192,384]{1,0:T(8,128)(2,1)S(1)} %shard_map.38), channel_id=1, source_target_pairs={{0,12},{4,8},{8,4},{12,0},{1,13},{5,9},{9,5},{13,1},{2,14},{6,10},... | collective-permute-start | bytes 442376 | tf_op jit(solution)/shard_map/ppermute | solution.py:224
  18.0 5.3 %collective-permute-start.1 = (bf16[192,384]{1,0:T(8,128)(2,1)S(1)}, bf16[192,384]{1,0:T(8,128)(2,1)S(1)}, u32[]{:S(2)}, u32[]{:S(2)}) collective-permute-start(bf16[192,384]{1,0:T(8,128)(2,1)S(1)} %collective-permute-done.mine), channel_id=1, source_target_pairs={{0,1},{1,0},{2,3},{3,2},{4,5},{5,4},{6,7},{7,6},{8,9},{9,8},{10,11... | collective-permute-start | bytes 442376 | tf_op jit(solution)/shard_map/ppermute | solution.py:255
  18.3 7.3 %collective-permute-start.5 = (bf16[320,384]{1,0:T(8,128)(2,1)S(1)}, bf16[320,384]{1,0:T(8,128)(2,1)S(1)}, u32[]{:S(2)}, u32[]{:S(2)}) collective-permute-start(bf16[320,384]{1,0:T(8,128)(2,1)S(1)} %shard_map.43.packed), channel_id=1, source_target_pairs={{0,1},{1,0},{2,3},{3,2},{4,5},{5,4},{6,7},{7,6},{8,9},{9,8},{10,11... | collective-permute-start | bytes 737288 | tf_op jit(solution)/shard_map/ppermute | solution.py:251
  21.8 3.7 %collective-permute-start.7 = (bf16[192,384]{1,0:T(8,128)(2,1)S(1)}, bf16[192,384]{1,0:T(8,128)(2,1)S(1)}, u32[]{:S(2)}, u32[]{:S(2)}) collective-permute-start(bf16[192,384]{1,0:T(8,128)(2,1)S(1)} %collective-permute-done.6.near), channel_id=1, source_target_pairs={{0,1},{1,0},{2,3},{3,2},{4,5},{5,4},{6,7},{7,6},{8,9},{9,8},{10,11... | collective-permute-start | bytes 442376 | tf_op jit(solution)/shard_map/ppermute | solution.py:255
  24.7 1.4 %copy-start.3 = (bf16[16,384,128]{2,1,0:T(8,128)(2,1)S(1)}, bf16[16,384,128]{2,1,0:T(8,128)(2,1)}, u32[]{:S(2)}) copy-start(bf16[16,384,128]{2,1,0:T(8,128)(2,1)} %u.3) | copy-start | bytes 4718596

commit v7 on v5

--- a/solution.py
+++ b/solution.py
@@ -51,9 +51,10 @@
         copy.wait()
 
 
-def take_near(index_of, src, out):
-    rows = out.shape[0]
-    out[...] = src[pl.ds(pl.multiple_of(index_of() * rows, rows), rows), :]
+def take_near(core_of, src, ours, theirs):
+    rows = ours.shape[0]
+    for out, index in ((ours, core_of()), (theirs, 1 - core_of())):
+        out[...] = src[pl.ds(pl.multiple_of(index * rows, rows), rows), :]
 
 
 def latent_part(first_j, r, u, out):
@@ -184,10 +185,13 @@
 
     def quarter_of():
         parity, core = spot()
-        return parity * 2 + core
+        return parity * 2 + 1 - core
 
     def across(i, k):
         return i ^ k if n_i & (n_i - 1) == 0 else (i + k) % n_i
+
+    def over(k):
+        return [(i * n_j + j, across(i, k) * n_j + (j ^ 1)) for i in range(n_i) for j in range(n_j)]
 
     core_swap = [(j, j ^ 1) for j in range(n_j)]
     chip_swap = [
@@ -203,10 +207,10 @@
         flops=2 * flops,
         moved=moved * 2 // 2,
     )(in_hbm(own))
-    piece = lax.ppermute(piece, "ia", [(i, across(i, far_away)) for i in range(n_i)])
-    rows = call(
+    piece = lax.ppermute(piece, ("ia", "ja"), over(far_away))
+    rows, other_rows = call(
         functools.partial(take_near, lambda: spot()[1]),
-        pltpu.VMEM((half, width), BF16),
+        (pltpu.VMEM((half, width), BF16), pltpu.VMEM((half, width), BF16)),
         [VMEM],
         flops=16 * flops,
         moved=8 * moved,
@@ -214,7 +218,10 @@
     near = {}
     for k in range(1, n_i):
         if k != far_away:
-            near[k] = lax.ppermute(rows, "ia", [(i, across(i, k)) for i in range(n_i)])
+            if k == 1:
+                near[k] = lax.ppermute(rows, "ia", [(i, across(i, k)) for i in range(n_i)])
+            else:
+                near[k] = lax.ppermute(other_rows, ("ia", "ja"), over(k))
 
     part = call(
         functools.partial(latent_part, first_j),

time: 24.6 us -> 25.6 us (1.041)
  starting transfers between devices: 11.2 us -> 13.7 us
  waiting for transfers between devices: 5.04 us -> 3.59 us
    ppermute x2 -> x1, starting transfers between devices: 4.97 us -> 1.64 us  [sigma_block(): near[k] = lax.ppermute(rows, 'ia', [(i, across(i, k)) for i in range(n_i)])]
    ppermute x2 -> x1, waiting for transfers between devices: 2.99 us -> 0.01 us  [sigma_block(): near[k] = lax.ppermute(rows, 'ia', [(i, across(i, k)) for i in range(n_i)])]
    ppermute x1 -> x2, starting transfers between devices: 4.15 us -> 6.74 us  [the longest x1 3.59 us: sigma_block(): piece = lax.ppermute(piece, ('ia', 'ja'), over(far_away))]
    ppermute x1 -> x2, waiting for transfers between devices: 1.69 us -> 3.57 us  [the longest x1 3.57 us: sigma_block(): near[k] = lax.ppermute(other_rows, ('ia', 'ja'), over(k))]
    ppermute x1, starting transfers between devices: 1.79 us -> 3.53 us  [sigma_block(): other = lax.ppermute(packed, ('grp', 'ja'), chip_swap)]
    ppermute x2, starting transfers between devices: 0.01 us -> 1.02 us  [sigma_block(): swapped[k] = lax.ppermute(mine, 'ja', core_swap)]
    ppermute x1, starting transfers between devices: 0.07 us -> 0.74 us  [sigma_block(): got = lax.ppermute(part, 'ja', core_swap)]
    ppermute x1, waiting for transfers between devices: 0.35 us -> 0.01 us  [sigma_block(): other = lax.ppermute(packed, ('grp', 'ja'), chip_swap)]
  transfers between devices with their start and end apart: 8 -> 8, of which waited for: 3 -> 1; matrix products, arithmetic and copies ran while one was open for 0% -> 0% of each run, Pallas kernels for 17% -> 17%
where the time goes in v7:
time: 25.6 us; the launch traced here: 25.5 us
  starting transfers between devices  13.7 us (54%)
  Pallas kernels  8.04 us (31%)
  waiting for transfers between devices  3.59 us (14%)
    ppermute x1, starting transfers between devices, sigma_block(): piece = lax.ppermute(piece, ('ia', 'ja'), over(far_away))  3.59 us
    ppermute x1, waiting for transfers between devices, sigma_block(): near[k] = lax.ppermute(other_rows, ('ia', 'ja'), over(k))  3.57 us
    ppermute x1, starting transfers between devices, sigma_block(): other = lax.ppermute(packed, ('grp', 'ja'), chip_swap)  3.53 us
    ppermute x1, starting transfers between devices, sigma_block(): near[k] = lax.ppermute(other_rows, ('ia', 'ja'), over(k))  3.14 us
    pallas_call x1, Pallas kernels, sigma_block(): call(functools.partial(ladder_last, spot, first_j, quarter), (jax.ShapeDt...  2.89 us
    ppermute x1, starting transfers between devices, sigma_block(): near[k] = lax.ppermute(rows, 'ia', [(i, across(i, k)) for i in range(n_i)])  1.64 us
    pallas_call x1, Pallas kernels, sigma_block(): call(functools.partial(ladder_near, spot), wide, [VMEM] * 4, [whole, half...  1.44 us
    pallas_call x1, Pallas kernels, sigma_block(): call(ladder_first, wide, [VMEM] * 2, [halfway], flops=2 * flops, moved=mo...  1.41 us
  transfers between devices with their start and end apart: 8, of which 1 were waited for; matrix products, arithmetic and copies ran while one was open for 0% of the time, Pallas kernels for 17%

profile of v7, /device:TPU:0, one launch (start us, length us, event | category | flops | bytes accessed | tf_op | source)
XLA Modules:
  0.0 25.5 jit_solution(4605647917378744996)
XLA Ops:
  0.0 0.0 copy-start.1
  0.0 0.0 copy-start
  0.0 0.0 copy-start.2
  0.0 0.9 %shard_map.41 = bf16[96,384]{1,0:T(8,128)(2,1)S(1)} custom-call(bf16[384,384]{1,0:T(8,128)(2,1)} %bitcast.8), custom_call_target="tpu_custom_call" | custom-call | flops 905969664 | bytes 1179648 | tf_op jit(solution)/shard_map/pallas_call | solution.py:202
  1.0 3.6 %collective-permute-start.3 = (bf16[96,384]{1,0:T(8,128)(2,1)S(1)}, bf16[96,384]{1,0:T(8,128)(2,1)S(1)}, u32[]{:S(2)}, u32[]{:S(2)}) collective-permute-start(bf16[96,384]{1,0:T(8,128)(2,1)S(1)} %shard_map.41), channel_id=1, source_target_pairs={{0,9},{1,8},{2,11},{3,10},{4,13},{5,12},{6,15},{7,14},{8,1},{9,0},... | collective-permute-start | bytes 221192 | tf_op jit(solution)/shard_map/ppermute | solution.py:210
  4.6 0.0 copy-done.1
  4.6 0.0 copy-done
  4.6 0.5 %shard_map.40.part = f32[384,128]{1,0:T(8,128)S(1)} custom-call(bf16[4,384,384]{2,1,0:T(8,128)(2,1)S(1)} %bitcast.3, bf16[16,384,128]{2,1,0:T(8,128)(2,1)S(1)} %copy-done.1), custom_call_target="tpu_custom_call" | custom-call | flops 150994944 | bytes 1179648 | tf_op jit(solution)/shard_map/pallas_call | solution.py:226
  5.0 0.7 %collective-permute-start.2 = (f32[384,128]{1,0:T(8,128)S(1)}, f32[384,128]{1,0:T(8,128)S(1)}, u32[]{:S(2)}, u32[]{:S(2)}) collective-permute-start(f32[384,128]{1,0:T(8,128)S(1)} %shard_map.40.part), channel_id=1, source_target_pairs={{0,1},{1,0},{2,3},{3,2},{4,5},{5,4},{6,7},{7,6},{8,9},{9,8},{10,11... | collective-permute-start | bytes 589832 | tf_op jit(solution)/shard_map/ppermute | solution.py:233
  5.8 0.0 copy-done.2
  5.8 1.6 %collective-permute-start = (bf16[192,384]{1,0:T(8,128)(2,1)S(1)}, bf16[192,384]{1,0:T(8,128)(2,1)S(1)}, u32[]{:S(2)}, u32[]{:S(2)}) collective-permute-start(bf16[192,384]{1,0:T(8,128)(2,1)S(1)} %get-tuple-element.8), channel_id=1, source_target_pairs={{0,4},{4,0},{8,12},{12,8},{1,5},{5,1},{9,13},{13,9},{2,6},{6,2},{1... | collective-permute-start | bytes 442376 | tf_op jit(solution)/shard_map/ppermute | solution.py:222
  7.4 0.0 collective-permute-done.3.piece
  7.4 0.0 collective-permute-done.2.got
  7.5 3.5 %collective-permute-start.4 = (bf16[224,384]{1,0:T(8,128)(2,1)S(1)}, bf16[224,384]{1,0:T(8,128)(2,1)S(1)}, u32[]{:S(2)}, u32[]{:S(2)}) collective-permute-start(bf16[224,384]{1,0:T(8,128)(2,1)S(1)} %shard_map.42.mine), channel_id=1, source_target_pairs={{0,2},{1,17},{2,0},{3,19},{16,18},{17,1},{18,16},{19,3},{4,6},{5,2... | collective-permute-start | bytes 516104 | tf_op jit(solution)/shard_map/ppermute | solution.py:241
  11.0 3.1 %collective-permute-start.6 = (bf16[192,384]{1,0:T(8,128)(2,1)S(1)}, bf16[192,384]{1,0:T(8,128)(2,1)S(1)}, u32[]{:S(2)}, u32[]{:S(2)}) collective-permute-start(bf16[192,384]{1,0:T(8,128)(2,1)S(1)} %get-tuple-element.9), channel_id=1, source_target_pairs={{0,13},{1,12},{2,15},{3,14},{4,9},{5,8},{6,11},{7,10},{8,5},{9,4},... | collective-permute-start | bytes 442376 | tf_op jit(solution)/shard_map/ppermute | solution.py:224
  14.2 0.0 collective-permute-done.mine
  14.2 0.7 %collective-permute-start.1 = (bf16[192,384]{1,0:T(8,128)(2,1)S(1)}, bf16[192,384]{1,0:T(8,128)(2,1)S(1)}, u32[]{:S(2)}, u32[]{:S(2)}) collective-permute-start(bf16[192,384]{1,0:T(8,128)(2,1)S(1)} %collective-permute-done.mine), channel_id=1, source_target_pairs={{0,1},{1,0},{2,3},{3,2},{4,5},{5,4},{6,7},{7,6},{8,9},{9,8},{10,11... | collective-permute-start | bytes 442376 | tf_op jit(solution)/shard_map/ppermute | solution.py:255
  14.9 0.0 collective-permute-done.4.theirs
  14.9 0.1 collective-permute-start.5
  15.0 3.6 %collective-permute-done.6.near = bf16[192,384]{1,0:T(8,128)(2,1)S(1)} collective-permute-done((bf16[192,384]{1,0:T(8,128)(2,1)S(1)}, bf16[192,384]{1,0:T(8,128)(2,1)S(1)}, u32[]{:S(2)}, u32[]{:S(2)}) %collective-permute-start.6) | collective-permute-done | bytes 147488 | tf_op jit(solution)/shard_map/ppermute | solution.py:224
  18.6 0.3 %collective-permute-start.7 = (bf16[192,384]{1,0:T(8,128)(2,1)S(1)}, bf16[192,384]{1,0:T(8,128)(2,1)S(1)}, u32[]{:S(2)}, u32[]{:S(2)}) collective-permute-start(bf16[192,384]{1,0:T(8,128)(2,1)S(1)} %collective-permute-done.6.near), channel_id=1, source_target_pairs={{0,1},{1,0},{2,3},{3,2},{4,5},{5,4},{6,7},{7,6},{8,9},{9,8},{10,11... | collective-permute-start | bytes 442376 | tf_op jit(solution)/shard_map/ppermute | solution.py:255
  18.9 1.4 %shard_map.37.acc = f32[384,1536]{1,0:T(8,128)S(1)} custom-call(bf16[4,384,384]{2,1,0:T(8,128)(2,1)S(1)} %bitcast.4, bf16[384,384]{1,0:T(8,128)(2,1)S(1)} %bitcast.10), custom_call_target="tpu_custom_call" | custom-call | flops 905969664 | bytes 1179648 | tf_op jit(solution)/shard_map/pallas_call | solution.py:238
  20.3 0.0 collective-permute-done.1.theirs
  20.3 1.4 %shard_map.39.acc = f32[384,1536]{1,0:T(8,128)S(1)} custom-call(f32[384,1536]{1,0:T(8,128)S(1)} %shard_map.37.acc, bf16[4,384,384]{2,1,0:T(8,128)(2,1)S(1)} %bitcast.5, bf16[192,384]{1,0:T(8,128)(2,1)S(1)} %collective-permute-done.mine, bf16[192,384]{1,0:T(8,128)(2,1)S(1)} %collective-permute-done.1.theirs), custom_call_target="tpu_custom_call", output_to_operand_aliasing={{}: (0, {})} | custom-call | flops 905969664 | bytes 1179648 | tf_op jit(solution)/shard_map/pallas_call | solution.py:258
  21.8 0.8 %shard_map.44.ahead = bf16[1536,768]{1,0:T(8,128)(2,1)S(1)} custom-call(bf16[4,384,384]{2,1,0:T(8,128)(2,1)S(1)} %bitcast.6, bf16[320,384]{1,0:T(8,128)(2,1)S(1)} %shard_map.43.packed, bf16[192,384]{1,0:T(8,128)(2,1)S(1)} %collective-permute-done.6.near), custom_call_target="tpu_custom_call" | custom-call | flops 452984832 | bytes 1179648 | tf_op jit(solution)/shard_map/pallas_call | solution.py:267
  22.6 0.0 collective-permute-done.7.swapped
  22.6 0.0 collective-permute-done.5.other
  22.6 2.9 %shard_map.45 = (bf16[4,384,384]{2,1,0:T(8,128)(2,1)}, bf16[1536,768]{1,0:T(8,128)(2,1)S(1)}) custom-call(f32[384,1536]{1,0:T(8,128)S(1)} %shard_map.39.acc, bf16[4,384,384]{2,1,0:T(8,128)(2,1)S(1)} %bitcast.7, bf16[320,384]{1,0:T(8,128)(2,1)S(1)} %shard_map.43.packed, ...), custom_call_target="tpu_custom_call", output_to_operand_aliasing={{1}: (7, {})} | custom-call | flops 1358954496 | bytes 2359296 | tf_op jit(solution)/shard_map/pallas_call | solution.py:274
  (3 shorter events, 0.1 us)
Async XLA Ops:
  0.0 4.6 %copy-start.1 = (bf16[16,384,128]{2,1,0:T(8,128)(2,1)S(1)}, bf16[16,384,128]{2,1,0:T(8,128)(2,1)}, u32[]{:S(2)}) copy-start(bf16[16,384,128]{2,1,0:T(8,128)(2,1)} %u.3) | copy-start | bytes 4718596
  0.0 4.6 %copy-start = (bf16[1,4,384,384]{3,2,1,0:T(8,128)(2,1)S(1)}, bf16[1,4,384,384]{3,2,1,0:T(8,128)(2,1)}, u32[]{:S(2)}) copy-start(bf16[1,4,384,384]{3,2,1,0:T(8,128)(2,1)} %param.3) | copy-start | bytes 3538948
  0.0 5.8 %copy-start.2 = (bf16[1,384,384]{2,1,0:T(8,128)(2,1)S(1)}, bf16[1,384,384]{2,1,0:T(8,128)(2,1)}, u32[]{:S(2)}) copy-start(bf16[1,384,384]{2,1,0:T(8,128)(2,1)} %param.4) | copy-start | bytes 884740
  1.0 6.5 %collective-permute-start.3 = (bf16[96,384]{1,0:T(8,128)(2,1)S(1)}, bf16[96,384]{1,0:T(8,128)(2,1)S(1)}, u32[]{:S(2)}, u32[]{:S(2)}) collective-permute-start(bf16[96,384]{1,0:T(8,128)(2,1)S(1)} %shard_map.41), channel_id=1, source_target_pairs={{0,9},{1,8},{2,11},{3,10},{4,13},{5,12},{6,15},{7,14},{8,1},{9,0},... | collective-permute-start | bytes 221192 | tf_op jit(solution)/shard_map/ppermute | solution.py:210
  5.0 2.4 %collective-permute-start.2 = (f32[384,128]{1,0:T(8,128)S(1)}, f32[384,128]{1,0:T(8,128)S(1)}, u32[]{:S(2)}, u32[]{:S(2)}) collective-permute-start(f32[384,128]{1,0:T(8,128)S(1)} %shard_map.40.part), channel_id=1, source_target_pairs={{0,1},{1,0},{2,3},{3,2},{4,5},{5,4},{6,7},{7,6},{8,9},{9,8},{10,11... | collective-permute-start | bytes 589832 | tf_op jit(solution)/shard_map/ppermute | solution.py:233
  5.8 8.4 %collective-permute-start = (bf16[192,384]{1,0:T(8,128)(2,1)S(1)}, bf16[192,384]{1,0:T(8,128)(2,1)S(1)}, u32[]{:S(2)}, u32[]{:S(2)}) collective-permute-start(bf16[192,384]{1,0:T(8,128)(2,1)S(1)} %get-tuple-element.8), channel_id=1, source_target_pairs={{0,4},{4,0},{8,12},{12,8},{1,5},{5,1},{9,13},{13,9},{2,6},{6,2},{1... | collective-permute-start | bytes 442376 | tf_op jit(solution)/shard_map/ppermute | solution.py:222
  7.5 7.4 %collective-permute-start.4 = (bf16[224,384]{1,0:T(8,128)(2,1)S(1)}, bf16[224,384]{1,0:T(8,128)(2,1)S(1)}, u32[]{:S(2)}, u32[]{:S(2)}) collective-permute-start(bf16[224,384]{1,0:T(8,128)(2,1)S(1)} %shard_map.42.mine), channel_id=1, source_target_pairs={{0,2},{1,17},{2,0},{3,19},{16,18},{17,1},{18,16},{19,3},{4,6},{5,2... | collective-permute-start | bytes 516104 | tf_op jit(solution)/shard_map/ppermute | solution.py:241
  11.0 7.6 %collective-permute-start.6 = (bf16[192,384]{1,0:T(8,128)(2,1)S(1)}, bf16[192,384]{1,0:T(8,128)(2,1)S(1)}, u32[]{:S(2)}, u32[]{:S(2)}) collective-permute-start(bf16[192,384]{1,0:T(8,128)(2,1)S(1)} %get-tuple-element.9), channel_id=1, source_target_pairs={{0,13},{1,12},{2,15},{3,14},{4,9},{5,8},{6,11},{7,10},{8,5},{9,4},... | collective-permute-start | bytes 442376 | tf_op jit(solution)/shard_map/ppermute | solution.py:224
  14.2 6.1 %collective-permute-start.1 = (bf16[192,384]{1,0:T(8,128)(2,1)S(1)}, bf16[192,384]{1,0:T(8,128)(2,1)S(1)}, u32[]{:S(2)}, u32[]{:S(2)}) collective-permute-start(bf16[192,384]{1,0:T(8,128)(2,1)S(1)} %collective-permute-done.mine), channel_id=1, source_target_pairs={{0,1},{1,0},{2,3},{3,2},{4,5},{5,4},{6,7},{7,6},{8,9},{9,8},{10,11... | collective-permute-start | bytes 442376 | tf_op jit(solution)/shard_map/ppermute | solution.py:255
  14.9 7.7 %collective-permute-start.5 = (bf16[320,384]{1,0:T(8,128)(2,1)S(1)}, bf16[320,384]{1,0:T(8,128)(2,1)S(1)}, u32[]{:S(2)}, u32[]{:S(2)}) collective-permute-start(bf16[320,384]{1,0:T(8,128)(2,1)S(1)} %shard_map.43.packed), channel_id=1, source_target_pairs={{0,1},{1,0},{2,3},{3,2},{4,5},{5,4},{6,7},{7,6},{8,9},{9,8},{10,11... | collective-permute-start | bytes 737288 | tf_op jit(solution)/shard_map/ppermute | solution.py:251
  18.6 4.0 %collective-permute-start.7 = (bf16[192,384]{1,0:T(8,128)(2,1)S(1)}, bf16[192,384]{1,0:T(8,128)(2,1)S(1)}, u32[]{:S(2)}, u32[]{:S(2)}) collective-permute-start(bf16[192,384]{1,0:T(8,128)(2,1)S(1)} %collective-permute-done.6.near), channel_id=1, source_target_pairs={{0,1},{1,0},{2,3},{3,2},{4,5},{5,4},{6,7},{7,6},{8,9},{9,8},{10,11... | collective-permute-start | bytes 442376 | tf_op jit(solution)/shard_map/ppermute | solution.py:255
